TPU v7x, 128 devices: a whole 4x4x4 slice. The times are simulated.
128 devices in a mesh: ao: 32 (over x, y, z_hi), aux: 4 (over z_lo, core).
Axes of the slice: x: 4, y: 4, z: 4 (z_hi: 2, z_lo: 2; z = z_hi * 2 + z_lo), core: 2. Of those that a mesh axis runs over, the one named last changes fastest.
Arguments:
- tensor: bfloat16 [64, 4096, 384], P('aux', 'ao'), may hold values from -0.15625 to 0.15625
- pattern: int32 [64, 96], P('aux', 'ao'), may hold values 0 or 1
- occ_density: bfloat16 [4096, 384], P('ao'), may hold values from -0.3125 to 0.3125
- virt_density: bfloat16 [4096, 384], P('ao'), may hold values from -0.3125 to 0.3125
Outputs:
- polarizability: float32 [64, 64], P('aux')
All inputs are finite; a program needn't handle non-finite values. No bound on the sum of `pattern` on one device may be relied on, other than what follows from the above.
Results may differ from a plain program's by a relative error of at most 0.0041.
Values may be sent and summed in bfloat16 or wider, within the bound.
A program may use at most 128 MiB of HBM per device.

v0:
```python
import jax
import jax.numpy as jnp
from jax import lax
from jax.sharding import PartitionSpec as P

AB = 128


def extended(cells, sides, width):
    for axis, dim in sides:
        count = lax.axis_size(axis)
        head = lax.slice_in_dim(cells, 0, width, axis=dim)
        tail = lax.slice_in_dim(cells, cells.shape[dim] - width, cells.shape[dim], axis=dim)
        cells = jnp.concatenate(
            [
                lax.ppermute(tail, axis, [(i, (i + 1) % count) for i in range(count)]),
                cells,
                lax.ppermute(head, axis, [((i + 1) % count, i) for i in range(count)]),
            ],
            axis=dim,
        )
    return cells


def copy_for_each(shard, axis):
    size = lax.axis_size(axis)
    return lax.all_to_all(
        jnp.broadcast_to(shard[None], (size, *shard.shape)), axis, 0, 0, tiled=True
    )


def taken_together(shard, axis):
    everything = copy_for_each(shard, axis)
    return jnp.sum(everything, axis=0)


def occ_side(masked, occ_rims, blocks):
    aux_count = masked.shape[0]
    factor_rows = masked.reshape(aux_count, blocks, AB, 3, AB)
    partner = occ_rims.reshape(blocks + 2, AB, 3, AB)
    pieces = [None] * 5
    for offset_a in range(3):
        for offset_b in range(3):
            term = jnp.einsum(
                "qlik,lkj->qlij",
                factor_rows[:, :, :, offset_a, :],
                partner[offset_a : offset_a + blocks, :, offset_b, :],
                preferred_element_type=jnp.float32,
            )
            slot = offset_a + offset_b
            pieces[slot] = term if pieces[slot] is None else pieces[slot] + term
    return jnp.stack(pieces, axis=3).astype(jnp.bfloat16).reshape(aux_count, -1)


def virt_side(virt_density, tensor_rims, blocks):
    aux_count = tensor_rims.shape[0]
    factor_rows = virt_density.reshape(blocks, AB, 3, AB)
    partner = tensor_rims.reshape(aux_count, blocks + 2, AB, 3, AB)
    pieces = [None] * 5
    for offset_a in range(3):
        for offset_b in range(3):
            term = jnp.einsum(
                "lik,qlkj->qlij",
                factor_rows[:, :, offset_a, :],
                partner[:, offset_a : offset_a + blocks, :, offset_b, :],
                preferred_element_type=jnp.float32,
            )
            slot = offset_a + offset_b
            pieces[slot] = term if pieces[slot] is None else pieces[slot] + term
    return jnp.stack(pieces, axis=3).astype(jnp.bfloat16).reshape(aux_count, -1)


def on_device(tensor, pattern, occ_density, virt_density):
    aux_count = tensor.shape[0]
    blocks = tensor.shape[1] // AB
    masked = (
        tensor.reshape(aux_count, blocks, AB, 3, AB)
        * pattern.reshape(aux_count, blocks, 1, 3, 1).astype(jnp.bfloat16)
    ).reshape(tensor.shape)
    occ_rims = extended(occ_density, (("ao", 0),), AB)
    occ_flat = occ_side(masked, occ_rims, blocks)
    own_rims = extended(masked, (("ao", 1),), AB)
    virt_flat = virt_side(virt_density, own_rims, blocks)
    columns = jnp.einsum(
        "pl,ql->pq",
        occ_flat,
        lax.all_gather(virt_flat, "aux", axis=0, tiled=True),
        preferred_element_type=jnp.float32,
    )
    return taken_together(columns, "ao")


def solution(mesh):
    return jax.shard_map(
        on_device,
        mesh=mesh,
        in_specs=(P("aux", "ao", None), P("aux", "ao"), P("ao", None), P("ao", None)),
        out_specs=P("aux", None),
        check_vma=False,
    )
```

profile of v0, /device:TPU:0, one launch (start us, length us, event | category | flops | bytes accessed | tf_op | source)
XLA Modules:
  0.0 297.3 jit_solution(1570233315929819093)
XLA Ops:
  6.5 0.7 convert_element_type.18
  7.5 1.6 broadcast_multiply_fusion
  9.0 8.7 %collective-permute-start.3 = (bf16[16,128,384]{2,1,0:T(8,128)(2,1)S(1)}, bf16[16,128,384]{2,1,0:T(8,128)(2,1)S(1)}, u32[]{:S(2)}, u32[]{:S(2)}) collective-permute-start(bf16[16,128,384]{2,1,0:T(8,128)(2,1)S(1)} %broadcast_multiply_fusion), channel_id=1, source_target_pairs={{4,0},{8,4},{12,8},{16,12},{20,16},{24,20},{28,24},{32,28},{36,32}... | collective-permute-start | bytes 4718600 | tf_op jit(solution)/shard_map/ppermute | solution.py:18
  17.8 63.3 %collective-permute-done.3 = bf16[16,128,384]{2,1,0:T(8,128)(2,1)S(1)} collective-permute-done((bf16[16,128,384]{2,1,0:T(8,128)(2,1)S(1)}, bf16[16,128,384]{2,1,0:T(8,128)(2,1)S(1)}, u32[]{:S(2)}, u32[]{:S(2)}) %collective-permute-start.3) | collective-permute-done | bytes 1572896 | tf_op jit(solution)/shard_map/ppermute | solution.py:18
  81.3 3.6 %pad_maximum_fusion = bf16[16,384,384]{2,1,0:T(8,128)(2,1)} fusion(bf16[16,128,384]{2,1,0:T(8,128)(2,1)S(1)} %collective-permute-done.3, bf16[16,128,384]{2,1,0:T(8,128)(2,1)S(1)} %broadcast_multiply_fusion, bf16[16,128,384]{2,1,0:T(8,128)(2,1)} %collective-permute-done.2), kind=kLoop, calls=%fused_computation | loop fusion | flops 14155776 | bytes 9437184 | tf_op jit(solution)/shard_map/concatenate | solution.py:14
  85.0 12.9 %reshape.260 = bf16[16,3,128,3,128]{4,3,2,1,0:T(4,128)(2,1)} reshape(bf16[16,384,384]{2,1,0:T(8,128)(2,1)} %pad_maximum_fusion) | data formatting | bytes 9437184 | tf_op jit(solution)/shard_map/reshape | solution.py:58
  97.9 14.0 %fusion.50 = (bf16[16,1,128,1,128]{4,3,2,1,0:T(2,128)(2,1)S(1)}, bf16[16,1,128,1,128]{4,3,2,1,0:T(2,128)(2,1)S(1)}, bf16[16,1,128,1,128]{4,3,2,1,0:T(2,128)(2,1)...) fusion(bf16[16,3,128,3,128]{4,3,2,1,0:T(4,128)(2,1)} %reshape.260), kind=kLoop, calls=%fused_computation.73 | loop fusion | bytes 9437184 | tf_op jit(solution)/shard_map/slice | solution.py:65
  111.9 3.5 %copy.69 = bf16[16,1,128,1,128]{2,4,0,3,1:T(8,128)(2,1)} copy(bf16[16,1,128,1,128]{4,3,2,1,0:T(2,128)(2,1)} %get-tuple-element.13) | data formatting | bytes 1048576
  115.4 3.5 %copy.71 = bf16[16,1,128,1,128]{2,4,0,3,1:T(8,128)(2,1)} copy(bf16[16,1,128,1,128]{4,3,2,1,0:T(2,128)(2,1)} %get-tuple-element.12) | data formatting | bytes 1048576
  118.8 2.1 fusion.11
  121.0 2.3 fusion.35
  123.3 3.5 %copy.72 = bf16[16,1,128,1,128]{2,4,0,3,1:T(8,128)(2,1)} copy(bf16[16,1,128,1,128]{4,3,2,1,0:T(2,128)(2,1)} %get-tuple-element.11) | data formatting | bytes 1048576
  126.7 3.5 %copy.74 = bf16[16,1,128,1,128]{2,4,0,3,1:T(8,128)(2,1)} copy(bf16[16,1,128,1,128]{4,3,2,1,0:T(2,128)(2,1)} %get-tuple-element.10) | data formatting | bytes 1048576
  130.2 2.3 fusion.32
  132.5 3.5 %copy.75 = bf16[16,1,128,1,128]{2,4,0,3,1:T(8,128)(2,1)} copy(bf16[16,1,128,1,128]{4,3,2,1,0:T(2,128)(2,1)} %get-tuple-element.9) | data formatting | bytes 1048576
  136.0 3.5 %copy.76 = bf16[16,1,128,1,128]{2,4,0,3,1:T(8,128)(2,1)} copy(bf16[16,1,128,1,128]{4,3,2,1,0:T(2,128)(2,1)} %get-tuple-element.8) | data formatting | bytes 1048576
  139.5 1.8 copy.78
  141.3 2.3 fusion.28
  143.6 1.8 copy.79
  145.4 0.7 copy.80
  146.1 1.7 convolution_add_fusion.2
  147.9 1.1 fusion.19
  148.9 1.1 fusion.17
  150.1 1.1 fusion.15
  151.1 1.1 fusion.13
  152.2 6.1 %copy.59 = bf16[16,1,128,5,128]{4,3,2,0,1:T(8,128)(2,1)} copy(bf16[16,1,128,5,128]{2,4,0,3,1:T(8,128)(2,1)} %fusion.13) | data formatting | bytes 5242880 | tf_op jit(solution)/shard_map/stack | solution.py:70
  158.3 5.5 %convert_element_type.20 = bf16[16,81920]{1,0:T(8,128)(2,1)} reshape(bf16[16,1,128,5,128]{4,3,2,0,1:T(8,128)(2,1)} %copy.59) | data formatting | bytes 5242880 | tf_op jit(solution)/shard_map/convert_element_type | solution.py:70
  163.8 0.9 copy-done.6
  164.7 8.0 %collective-permute-start.1 = (bf16[128,384]{1,0:T(8,128)(2,1)S(1)}, bf16[128,384]{1,0:T(8,128)(2,1)S(1)}, u32[]{:S(2)}, u32[]{:S(2)}) collective-permute-start(bf16[128,384]{1,0:T(8,128)(2,1)S(1)} %copy-done.6), channel_id=1, source_target_pairs={{4,0},{8,4},{12,8},{16,12},{20,16},{24,20},{28,24},{32,28},{36,32}... | collective-permute-start | bytes 294920 | tf_op jit(solution)/shard_map/ppermute | solution.py:18
  172.7 1.6 copy.34
  174.3 2.0 copy.35
  176.5 6.6 %collective-permute-done = bf16[128,384]{1,0:T(8,128)(2,1)S(1)} collective-permute-done((bf16[128,384]{1,0:T(8,128)(2,1)S(1)}, bf16[128,384]{1,0:T(8,128)(2,1)S(1)}, u32[]{:S(2)}, u32[]{:S(2)}) %collective-permute-start) | collective-permute-done | bytes 98336 | tf_op jit(solution)/shard_map/ppermute | solution.py:16
  183.2 0.5 fusion.51
  184.9 1.1 fusion.7
  186.3 0.3 fusion.38
  186.6 0.3 fusion.40
  186.9 1.1 fusion.25
  188.3 1.1 fusion.23
  189.4 1.1 fusion.21
  190.5 1.1 fusion.9
  191.6 6.1 %copy.44 = bf16[16,1,128,5,128]{4,3,2,0,1:T(8,128)(2,1)} copy(bf16[16,1,128,5,128]{2,4,0,3,1:T(8,128)(2,1)} %fusion.9) | data formatting | bytes 5242880 | tf_op jit(solution)/shard_map/stack | solution.py:52
  197.8 4.5 %convert_element_type.19 = bf16[16,81920]{1,0:T(8,128)(2,1)S(1)} reshape(bf16[16,1,128,5,128]{4,3,2,0,1:T(8,128)(2,1)} %copy.44) | data formatting | bytes 5242880 | tf_op jit(solution)/shard_map/convert_element_type | solution.py:52
  202.2 61.1 %all-gather.2.cloned.1.call-done = bf16[64,81920]{1,0:T(8,128)(2,1)} async-done(((bf16[16,81920]{1,0:T(8,128)(2,1)}), bf16[64,81920]{1,0:T(8,128)(2,1)}) %all-gather.2.cloned.1.call-update) | async-done | bytes 10485776 | tf_op jit(solution)/shard_map/all_gather | solution.py:87
  263.3 5.5 %fusion.52 = f32[16,64]{1,0:T(8,128)S(1)} fusion(bf16[16,81920]{1,0:T(8,128)(2,1)S(1)} %convert_element_type.19, bf16[64,81920]{1,0:T(8,128)(2,1)} %all-gather.2.cloned.1.call-done), kind=kOutput, calls=%fused_computation.75 | convolution fusion | flops 167772160 | bytes 13111296 | tf_op jit(solution)/shard_map/pl,ql->pq/dot_general | solution.py:84
  269.0 19.2 %all_to_all.5 = f32[32,1,1024]{2,1,0:T(1,128)S(1)} all-to-all(f32[32,1,1024]{2,1,0:T(1,128)S(1)} %reshape.286), channel_id=1, replica_groups=mesh['ao'=32,'aux'=4] {'ao'}, dimensions={0} | all-to-all | bytes 262144 | tf_op jit(solution)/shard_map/all_to_all | solution.py:27
  288.3 0.5 broadcast.13
  288.8 0.9 reduce
  289.8 0.6 reduce_sum.9
  (42 shorter events, 2.8 us)
Async XLA Ops:
  6.5 11.2 %copy-start.7 = (bf16[128,384]{1,0:T(8,128)(2,1)S(1)}, bf16[128,384]{1,0:T(8,128)(2,1)}, u32[]{:S(2)}) copy-start(bf16[128,384]{1,0:T(8,128)(2,1)} %param.7) | copy-start | bytes 294916
  6.5 256.8 %all-gather.2.cloned.1.call-start = ((), (), s32[]{:S(2)}) async-start(), calls=%async_computation.1 | async-start | bytes 13107200 | tf_op jit(solution)/shard_map/all_gather | solution.py:87
  9.0 72.1 %collective-permute-start.3 = (bf16[16,128,384]{2,1,0:T(8,128)(2,1)S(1)}, bf16[16,128,384]{2,1,0:T(8,128)(2,1)S(1)}, u32[]{:S(2)}, u32[]{:S(2)}) collective-permute-start(bf16[16,128,384]{2,1,0:T(8,128)(2,1)S(1)} %broadcast_multiply_fusion), channel_id=1, source_target_pairs={{4,0},{8,4},{12,8},{16,12},{20,16},{24,20},{28,24},{32,28},{36,32}... | collective-permute-start | bytes 4718600 | tf_op jit(solution)/shard_map/ppermute | solution.py:18
  17.7 63.6 %collective-permute-start.2 = (bf16[16,128,384]{2,1,0:T(8,128)(2,1)S(1)}, bf16[16,128,384]{2,1,0:T(8,128)(2,1)}, u32[]{:S(2)}, u32[]{:S(2)}) collective-permute-start(bf16[16,128,384]{2,1,0:T(8,128)(2,1)S(1)} %broadcast_multiply_fusion), channel_id=1, source_target_pairs={{0,4},{4,8},{8,12},{12,16},{16,20},{20,24},{24,28},{28,32},{32,36}... | collective-permute-start | bytes 4718600 | tf_op jit(solution)/shard_map/ppermute | solution.py:16
  143.6 4.2 %copy-start.1 = (f32[16,128,128]{2,1,0:T(8,128)S(1)}, f32[16,128,128]{2,1,0:T(8,128)}, u32[]{:S(2)}) copy-start(f32[16,128,128]{2,1,0:T(8,128)} %fusion.35) | copy-start | bytes 3145732
  145.4 2.5 copy-start.3
  146.1 2.9 copy-start.4
  147.8 2.2 copy-start.2
  147.8 2.2 copy-start.5
  163.8 0.9 copy-start.6
  163.8 8.9 %copy-start = (bf16[16,128,384]{2,1,0:T(8,128)(2,1)S(1)}, bf16[16,128,384]{2,1,0:T(8,128)(2,1)}, u32[]{:S(2)}) copy-start(bf16[16,128,384]{2,1,0:T(8,128)(2,1)} %param.4) | copy-start | bytes 4718596
  164.7 11.8 %collective-permute-start.1 = (bf16[128,384]{1,0:T(8,128)(2,1)S(1)}, bf16[128,384]{1,0:T(8,128)(2,1)S(1)}, u32[]{:S(2)}, u32[]{:S(2)}) collective-permute-start(bf16[128,384]{1,0:T(8,128)(2,1)S(1)} %copy-done.6), channel_id=1, source_target_pairs={{4,0},{8,4},{12,8},{16,12},{20,16},{24,20},{28,24},{32,28},{36,32}... | collective-permute-start | bytes 294920 | tf_op jit(solution)/shard_map/ppermute | solution.py:18
  172.7 10.4 %collective-permute-start = (bf16[128,384]{1,0:T(8,128)(2,1)S(1)}, bf16[128,384]{1,0:T(8,128)(2,1)S(1)}, u32[]{:S(2)}, u32[]{:S(2)}) collective-permute-start(bf16[128,384]{1,0:T(8,128)(2,1)S(1)} %copy-done.6), channel_id=1, source_target_pairs={{0,4},{4,8},{8,12},{12,16},{16,20},{20,24},{24,28},{28,32},{32,36}... | collective-permute-start | bytes 294920 | tf_op jit(solution)/shard_map/ppermute | solution.py:16
Sparse Core Ops, SparseCore 0:
  163.9 99.3 all-gather.1
where the time goes:
time: 300 us; the launch traced here: 297 us
  waiting for transfers between devices  131 us (44%)
  local copies, waits for them, and re-layouts  81.5 us (27%)
  matrix products  27.3 us (9%)
  blocking collectives  19.2 us (6%)
  starting transfers between devices  16.7 us (6%)
  between operations  13.6 us (5%)
  other arithmetic  7.71 us (3%)
    ppermute x2, waiting for transfers between devices, extended(): lax.ppermute(head, axis, [((i + 1) % count, i) for i in range(count)])  63.3 us
    all_gather x1, waiting for transfers between devices, on_device(): lax.all_gather(virt_flat, 'aux', axis=0, tiled=True)  61.1 us
    unnamed x39, local copies, waits for them, and re-layouts  29.1 us
    all_to_all x1, blocking collectives, copy_for_each(): lax.all_to_all(jnp.broadcast_to(shard[None], (size, *shard.shape)), axis,...  19.2 us
    ppermute x2, starting transfers between devices, extended(): lax.ppermute(head, axis, [((i + 1) % count, i) for i in range(count)])  16.7 us
    dot_general x9, matrix products, virt_side(): jnp.einsum('lik,qlkj->qlij', factor_rows[:, :, offset_a, :], partner[:, o...  15.1 us
    slice x1, local copies, waits for them, and re-layouts, virt_side(): partner[:, offset_a:offset_a + blocks, :, offset_b, :]  14 us
    reshape x1, local copies, waits for them, and re-layouts, virt_side(): partner = tensor_rims.reshape(aux_count, blocks + 2, AB, 3, AB)  12.9 us
  transfers between devices with their start and end apart: 5, of which 4 were waited for; matrix products, arithmetic and copies ran while one was open for 8% of the time, Pallas kernels for 0%

commit v1 on v0

v1 whole, which is shorter than its diff:
```python
import functools

import jax
import jax.numpy as jnp
from jax import lax
from jax.experimental import pallas as pl
from jax.experimental.pallas import tpu as pltpu
from jax.sharding import PartitionSpec as P

MESH = pl.DeviceIdType.MESH
AB = 128
PA = 16
W = 3 * AB
NG = 8
GR = AB // NG
NS = 4
PS = PA // NS
F32 = jnp.float32
BF16 = jnp.bfloat16


def rows(g, size):
    return pl.ds(pl.multiple_of(g * size, size), size)


def side(refs, base):
    return jnp.concatenate(
        [jnp.concatenate([ref[base + u] for ref in refs], axis=0) for u in range(GR)], axis=1
    )


def gram(left, right):
    return lax.dot_general(left, right, (((1,), (1,)), ((), ())), preferred_element_type=F32)


def padded(x):
    return jnp.concatenate([x, jnp.zeros((x.shape[0], 128 - x.shape[1]), F32)], axis=1)


def kernel(
    n_ao,
    tensor, pattern, occ, virt, out,
    own_nat, own_row, mate_nat, mate_row, near, far, t_sib, t_own, t_mate, t_nat, mask, occ_rims, occ_wide, virt_t,
    acc_own, acc_mate, acc_near, acc_third, pair_send, pair_recv, sum_a, sum_b,
    in_sem, occ_ss, occ_rs, near_ss, near_rs, mate_ss, mate_rs, far_ss, far_rs, nsib_ss, nsib_rs, fsib_ss, fsib_rs,
    t_ss, t_rs, pair_ss, pair_rs, a_ss, a_rs, b_ss, b_rs,
):
    l, a = lax.axis_index("ao"), lax.axis_index("aux")
    zl, c = lax.div(a, 2), lax.rem(a, 2)
    zh = lax.rem(l, 2)
    flip = (1 - zl) * 2 + c
    up, down = lax.rem(l + 1, n_ao), lax.rem(l + n_ao - 1, n_ao)
    mate = (l, flip)
    cross = (l + 1 - 2 * zh, flip)
    sib = (l, zl * 2 + 1 - c)
    onward = (lax.rem(l + n_ao + 2 - 4 * zh, n_ao), a)
    backward = (lax.rem(l + n_ao - 2 + 4 * zh, n_ao), a)
    gx, gr = lax.div(l, 8), lax.rem(l, 8)
    n_x = n_ao // 8

    def peer_a(d):
        return gx * 8 + lax.rem(gr + d, 8)

    def peer_b(d):
        return lax.rem(gx + d, n_x) * 8 + gr

    def copy(src, dst, ss, rs, to):
        return pltpu.make_async_remote_copy(
            src_ref=src, dst_ref=dst, send_sem=ss, recv_sem=rs, device_id=to, device_id_type=MESH
        )

    def load(g):
        return pltpu.make_async_copy(tensor.at[:, rows(g, GR), :], own_nat.at[:, rows(g, GR), :], in_sem.at[g])

    def send_near(g):
        return copy(own_row.at[rows(g, GR)], near.at[c, rows(g, GR)], near_ss.at[g], near_rs.at[g], cross)

    def send_mate(s):
        return copy(own_nat.at[rows(s, PS)], mate_nat.at[rows(s, PS)], mate_ss.at[s], mate_rs.at[s], mate)

    def send_far(g):
        return copy(near.at[c, rows(g, GR)], far.at[c, rows(g, GR)], far_ss.at[g], far_rs.at[g], onward)

    def near_sib(g, core):
        return copy(near.at[core, rows(g, GR)], near.at[core, rows(g, GR)], nsib_ss.at[g], nsib_rs.at[g], sib)

    def far_sib(g, core):
        return copy(far.at[core, rows(g, GR)], far.at[core, rows(g, GR)], fsib_ss.at[g], fsib_rs.at[g], sib)

    @pl.loop(0, NG)
    def _(g):
        load(g).start()

    barrier = pltpu.get_barrier_semaphore()
    greeted = [mate, sib, (up, flip), (down, flip), onward, backward]
    greeted += [(peer_a(d), a) for d in range(1, 8)] + [(peer_b(d), a) for d in range(1, n_x)]
    for other in greeted:
        pl.semaphore_signal(barrier, inc=1, device_id=other, device_id_type=MESH)

    for p in range(PA):
        for o in range(3):
            kept = pattern[p, o].astype(F32)
            mask[p, :, o * AB : (o + 1) * AB] = jnp.full((GR, AB), kept, F32).astype(BF16)
    for j in range(3):
        virt_t[j] = virt[:, j * AB : (j + 1) * AB].astype(F32).T.astype(BF16)
    occ_wide[...] = jnp.zeros_like(occ_wide)
    occ_wide[AB:, AB:] = occ[...]
    for acc in (acc_own, acc_mate, acc_near, acc_third):
        acc[...] = jnp.zeros_like(acc)

    pl.semaphore_wait(barrier, len(greeted))

    to_up = copy(occ, occ_rims.at[0], occ_ss.at[0], occ_rs.at[0], (up, flip))
    to_down = copy(occ, occ_rims.at[1], occ_ss.at[1], occ_rs.at[1], (down, flip))
    to_up.start()
    to_down.start()

    @pl.loop(0, NG)
    def _(g):
        load(g).wait()
        kept = own_nat[:, rows(g, GR), :] * mask[...]
        own_nat[:, rows(g, GR), :] = kept
        own_row[rows(g, GR)] = jnp.swapaxes(kept, 0, 1)
        send_near(g).start()

    @pl.loop(0, NS)
    def _(s):
        send_mate(s).start()

    to_up.wait_recv()
    to_down.wait_recv()
    occ_wide[:AB, :W] = occ_rims[0]

    def transform(nat, s, offsets):
        x = nat[rows(s, PS)].reshape(PS * AB, W)
        first = jnp.dot(x[:, : 2 * AB], occ_wide[...], preferred_element_type=F32)
        second = jnp.dot(x[:, 2 * AB :], occ_rims[1], preferred_element_type=F32)
        side_occ = jnp.concatenate(
            [first[:, : 2 * AB], first[:, 2 * AB :] + second[:, : 2 * AB], second[:, 2 * AB :]], axis=1
        ).astype(BF16)
        for q in range(PS):
            block = side_occ[q * AB : (q + 1) * AB]
            for j in offsets:
                part = jnp.dot(virt_t[j], block[:, j * AB : j * AB + W], preferred_element_type=F32)
                t_nat[j, s * PS + q] = part.astype(BF16)

    def to_rows(nat, dst, g):
        dst[rows(g, GR)] = jnp.swapaxes(nat[:, rows(g, GR), :], 0, 1)

    def pass_on(g):
        send_near(g).wait_recv()
        send_far(g).start()
        near_sib(g, c).start()

    @pl.loop(0, NS)
    def _(s):
        transform(own_nat, s, (0, 1, 2))

    @pl.loop(0, NG)
    def _(g):
        for j in range(3):
            to_rows(t_nat.at[j], t_own.at[j], g)

    share = copy(t_own.at[1], t_sib, t_ss, t_rs, sib)
    share.start()
    inward, outward = 2 - 2 * zh, 2 * zh
    t_in, t_out = t_own.at[inward], t_own.at[outward]
    m_in, m_out = t_mate.at[inward], t_mate.at[outward]
    near_both = [near.at[0], near.at[1]]
    far_both = [far.at[0], far.at[1]]

    def use_near(g):
        near_sib(g, 1 - c).wait_recv()
        acc_near[...] += gram(side([t_in], g * GR), side(near_both, g * GR))

    def take_far(g):
        send_far(g).wait_recv()
        far_sib(g, c).start()

    def use_far(g):
        far_sib(g, 1 - c).wait_recv()
        acc_near[...] += gram(side([t_out], g * GR), side(far_both, g * GR))

    pass_on(0)
    share.wait_recv()

    @pl.loop(0, NG)
    def _(g):
        @pl.when(g + 1 < NG)
        def _():
            pass_on(g + 1)

        acc_own[...] += gram(side([t_own.at[1], t_sib], g * GR), side([own_row], g * GR))
        use_near(g)

        @pl.when(lax.rem(g, 2) == 1)
        def _():
            s = lax.div(g, 2)
            send_mate(s).wait_recv()
            transform(mate_nat, s, (0, 2))

        @pl.when(g >= 1)
        def _():
            take_far(g - 1)

        @pl.when(g >= 2)
        def _():
            use_far(g - 2)

    @pl.loop(0, NG)
    def _(g):
        for j in (0, 2):
            to_rows(t_nat.at[j], t_mate.at[j], g)
        to_rows(mate_nat, mate_row, g)
        acc_mate[...] += gram(side([t_own.at[1], t_sib], g * GR), side([mate_row], g * GR))

    take_far(NG - 1)
    use_far(NG - 2)

    @pl.loop(0, NG)
    def _(g):
        acc_third[...] += gram(side([m_in], g * GR), side(near_both, g * GR))

    @pl.loop(0, NG)
    def _(g):
        @pl.when(g == NG - 1)
        def _():
            use_far(NG - 1)

        acc_third[...] += gram(side([m_out], g * GR), side(far_both, g * GR))

    pair_send[0] = padded(jnp.concatenate([acc_own[PA:], acc_mate[PA:]], axis=1))
    pair_send[1] = padded(acc_third[...])
    to_sib = copy(pair_send.at[0], pair_recv.at[0], pair_ss.at[0], pair_rs.at[0], sib)
    to_mate = copy(pair_send.at[1], pair_recv.at[1], pair_ss.at[1], pair_rs.at[1], mate)
    to_sib.start()
    to_mate.start()
    to_sib.wait_recv()
    to_mate.wait_recv()

    def by_core(mine, theirs):
        return jnp.where(
            c == 0, jnp.concatenate([mine, theirs], axis=1), jnp.concatenate([theirs, mine], axis=1)
        )

    from_sib, from_mate = pair_recv[0], pair_recv[1]
    same = by_core(acc_own[:PA], from_sib[:, :PA]) + from_mate[:, : 2 * PA]
    other = by_core(acc_mate[:PA], from_sib[:, PA : 2 * PA]) + acc_near[...]
    whole = jnp.where(
        zl == 0, jnp.concatenate([same, other], axis=1), jnp.concatenate([other, same], axis=1)
    )

    def exchange(value, slots, me, count, ss, rs, peer, other_index):
        slots[me] = value
        for d in range(1, count):
            copy(slots.at[me], slots.at[me], ss.at[d], rs.at[me], (peer(d), a)).start()
        for d in range(1, count):
            slot = other_index(d)
            copy(slots.at[slot], slots.at[slot], ss.at[d], rs.at[slot], (peer(d), a)).wait_recv()
        total = slots[0]
        for i in range(1, count):
            total = total + slots[i]
        return total

    part = exchange(padded(whole), sum_a, gr, 8, a_ss, a_rs, peer_a, lambda d: lax.rem(gr + d, 8))
    total = exchange(part, sum_b, gx, n_x, b_ss, b_rs, peer_b, lambda d: lax.rem(gx + d, n_x))
    out[...] = total[:, : 4 * PA]

    to_up.wait_send()
    to_down.wait_send()
    share.wait_send()
    to_sib.wait_send()
    to_mate.wait_send()

    @pl.loop(0, NG)
    def _(g):
        send_near(g).wait_send()
        send_far(g).wait_send()
        near_sib(g, c).wait_send()
        far_sib(g, c).wait_send()

    @pl.loop(0, NS)
    def _(s):
        send_mate(s).wait_send()

    for d in range(1, 8):
        copy(sum_a.at[gr], sum_a.at[gr], a_ss.at[d], a_rs.at[gr], (peer_a(d), a)).wait_send()
    for d in range(1, n_x):
        copy(sum_b.at[gx], sum_b.at[gx], b_ss.at[d], b_rs.at[gx], (peer_b(d), a)).wait_send()


def solution(mesh):
    n_ao = mesh.shape["ao"]
    dma = pltpu.SemaphoreType.DMA
    row = (AB, PA, W)
    nat = (PA, AB, W)
    vmem = pl.BlockSpec(memory_space=pltpu.VMEM)

    def on_device(tensor, pattern, occ, virt):
        return pl.pallas_call(
            functools.partial(kernel, n_ao),
            out_shape=jax.ShapeDtypeStruct((PA, 4 * PA), F32),
            in_specs=[
                pl.BlockSpec(memory_space=pl.ANY),
                pl.BlockSpec(memory_space=pltpu.SMEM),
                vmem,
                vmem,
            ],
            out_specs=vmem,
            scratch_shapes=[
                pltpu.VMEM(nat, BF16),
                pltpu.VMEM(row, BF16),
                pltpu.VMEM(nat, BF16),
                pltpu.VMEM(row, BF16),
                pltpu.VMEM((2, *row), BF16),
                pltpu.VMEM((2, *row), BF16),
                pltpu.VMEM(row, BF16),
                pltpu.VMEM((3, *row), BF16),
                pltpu.VMEM((3, *row), BF16),
                pltpu.VMEM((3, *nat), BF16),
                pltpu.VMEM((PA, GR, W), BF16),
                pltpu.VMEM((2, AB, W), BF16),
                pltpu.VMEM((2 * AB, 4 * AB), BF16),
                pltpu.VMEM((3, AB, AB), BF16),
                pltpu.VMEM((2 * PA, PA), F32),
                pltpu.VMEM((2 * PA, PA), F32),
                pltpu.VMEM((PA, 2 * PA), F32),
                pltpu.VMEM((PA, 2 * PA), F32),
                pltpu.VMEM((2, PA, 128), F32),
                pltpu.VMEM((2, PA, 128), F32),
                pltpu.VMEM((8, PA, 128), F32),
                pltpu.VMEM((n_ao // 8, PA, 128), F32),
                dma((NG,)),
                dma((2,)),
                dma((2,)),
                dma((NG,)),
                dma((NG,)),
                dma((NS,)),
                dma((NS,)),
                dma((NG,)),
                dma((NG,)),
                dma((NG,)),
                dma((NG,)),
                dma((NG,)),
                dma((NG,)),
                dma(()),
                dma(()),
                dma((2,)),
                dma((2,)),
                dma((8,)),
                dma((8,)),
                dma((n_ao // 8,)),
                dma((n_ao // 8,)),
            ],
            compiler_params=pltpu.CompilerParams(
                collective_id=0, has_side_effects=True, vmem_limit_bytes=52 << 20
            ),
        )(tensor, pattern, occ, virt)

    return jax.shard_map(
        on_device,
        mesh=mesh,
        in_specs=(P("aux", "ao", None), P("aux", "ao"), P("ao", None), P("ao", None)),
        out_specs=P("aux", None),
        check_vma=False,
    )
```

time: 300 us -> 77.6 us (0.26)
  waiting for transfers between devices: 131 us -> 0 us
  local copies, waits for them, and re-layouts: 81.5 us -> 4.55 us
  Pallas kernels: 0 us -> 72.8 us
  matrix products: 27.3 us -> 0 us
  blocking collectives: 19.2 us -> 0 us
  starting transfers between devices: 16.7 us -> 0 us
  between operations: 13.6 us -> 0.01 us
  other arithmetic: 7.71 us -> 0 us
    pallas_call x0 -> x1, Pallas kernels: none -> 72.8 us  [on_device(): pl.pallas_call(functools.partial(kernel, n_ao), out_shape=jax.ShapeDtypeS...]
    ppermute x4 -> x0, waiting for transfers between devices: 70.1 us -> none  [the longest x2 63.3 us: extended(): lax.ppermute(head, axis, [((i + 1) % count, i) for i in range(count)])]
    all_gather x1 -> x0, waiting for transfers between devices: 61.1 us -> none  [on_device(): lax.all_gather(virt_flat, 'aux', axis=0, tiled=True)]
    dot_general x19 -> x0, matrix products: 27.3 us -> none  [the longest x9 15.1 us: virt_side(): jnp.einsum('lik,qlkj->qlij', factor_rows[:, :, offset_a, :], partner[:, o...]
    unnamed x39 -> x8, local copies, waits for them, and re-layouts: 29.1 us -> 4.55 us
    all_to_all x1 -> x0, blocking collectives: 19.2 us -> none  [copy_for_each(): lax.all_to_all(jnp.broadcast_to(shard[None], (size, *shard.shape)), axis,...]
    ppermute x4 -> x0, starting transfers between devices: 16.7 us -> none  [the longest x2 16.7 us: extended(): lax.ppermute(head, axis, [((i + 1) % count, i) for i in range(count)])]
    reshape x3 -> x0, local copies, waits for them, and re-layouts: 15 us -> none  [the longest x1 12.9 us: virt_side(): partner = tensor_rims.reshape(aux_count, blocks + 2, AB, 3, AB)]
  transfers between devices with their start and end apart: 5 -> 0, of which waited for: 4 -> 0; matrix products, arithmetic and copies ran while one was open for 8% -> 0% of each run, Pallas kernels for 0% -> 0%
where the time goes in v1:
time: 77.6 us; the launch traced here: 77.4 us
  Pallas kernels  72.8 us (94%)
  local copies, waits for them, and re-layouts  4.55 us (6%)
    pallas_call x1, Pallas kernels, on_device(): pl.pallas_call(functools.partial(kernel, n_ao), out_shape=jax.ShapeDtypeS...  72.8 us
    unnamed x8, local copies, waits for them, and re-layouts  4.55 us

profile of v1, /device:TPU:0, one launch (start us, length us, event | category | flops | bytes accessed | tf_op | source)
XLA Modules:
  0.0 77.4 jit_solution(2497573809292633542)
XLA Ops:
  0.0 0.8 copy.5.pattern
  0.8 0.0 copy-start
  0.8 1.4 %copy-done = bf16[16,128,384]{2,1,0:T(8,128)(2,1)S(1)} copy-done((bf16[16,128,384]{2,1,0:T(8,128)(2,1)S(1)}, bf16[16,128,384]{2,1,0:T(8,128)(2,1)}, u32[]{:S(2)}) %copy-start) | copy-done | bytes 1572888
  2.2 0.0 copy-start.1
  2.2 0.9 %copy-done.1 = bf16[128,384]{1,0:T(8,128)(2,1)S(1)} copy-done((bf16[128,384]{1,0:T(8,128)(2,1)S(1)}, bf16[128,384]{1,0:T(8,128)(2,1)}, u32[]{:S(2)}) %copy-start.1) | copy-done | bytes 98328
  3.1 0.0 copy-start.2
  3.1 0.9 %copy-done.2 = bf16[128,384]{1,0:T(8,128)(2,1)S(1)} copy-done((bf16[128,384]{1,0:T(8,128)(2,1)S(1)}, bf16[128,384]{1,0:T(8,128)(2,1)}, u32[]{:S(2)}) %copy-start.2) | copy-done | bytes 98328
  4.0 72.8 %shard_map.46 = f32[16,64]{1,0:T(8,128)S(1)} custom-call(bf16[16,128,384]{2,1,0:T(8,128)(2,1)S(1)} %copy-done, s32[16,3]{1,0:T(8,128)S(1)} %copy.5.pattern, bf16[128,384]{1,0:T(8,128)(2,1)S(1)} %copy-done.1, bf16[128,384]{1,0:T(8,128)(2,1)S(1)} %copy-done.2), custom_call_target="tpu_custom_call" | custom-call | tf_op jit(solution)/shard_map/pallas_call | solution.py:300
  76.8 0.6 copy.7
Async XLA Ops:
  0.8 1.4 %copy-start = (bf16[16,128,384]{2,1,0:T(8,128)(2,1)S(1)}, bf16[16,128,384]{2,1,0:T(8,128)(2,1)}, u32[]{:S(2)}) copy-start(bf16[16,128,384]{2,1,0:T(8,128)(2,1)} %tensor.1) | copy-start | bytes 4718596
  2.2 0.9 %copy-start.1 = (bf16[128,384]{1,0:T(8,128)(2,1)S(1)}, bf16[128,384]{1,0:T(8,128)(2,1)}, u32[]{:S(2)}) copy-start(bf16[128,384]{1,0:T(8,128)(2,1)} %occ.1) | copy-start | bytes 294916
  3.1 0.9 %copy-start.2 = (bf16[128,384]{1,0:T(8,128)(2,1)S(1)}, bf16[128,384]{1,0:T(8,128)(2,1)}, u32[]{:S(2)}) copy-start(bf16[128,384]{1,0:T(8,128)(2,1)} %virt.1) | copy-start | bytes 294916

commit v2 on v1

v2 whole, which is shorter than its diff:
```python
import functools

import jax
import jax.numpy as jnp
from jax import lax
from jax.experimental import pallas as pl
from jax.experimental.pallas import tpu as pltpu
from jax.sharding import PartitionSpec as P

MESH = pl.DeviceIdType.MESH
AB = 128
PA = 16
W = 3 * AB
NG = 8
GR = AB // NG
PS = 4
F32 = jnp.float32
BF16 = jnp.bfloat16


def rows(g, size):
    return pl.ds(pl.multiple_of(g * size, size), size)


def side(refs, g, count=GR):
    return jnp.concatenate(
        [jnp.concatenate([ref[g * count + u] for ref in refs], axis=0) for u in range(count)], axis=1
    )


def gram(left, right):
    return lax.dot_general(left, right, (((1,), (1,)), ((), ())), preferred_element_type=F32)


def folded(x):
    return jnp.concatenate([x[:8], x[8:]], axis=1)


def kernel(
    n_ao,
    tensor_hbm, pattern_hbm, occ_hbm, virt_hbm, out,
    pattern, occ, virt,
    own_nat, own_row, mate_row, near, far, t_sib, t_own, t_mate, t_nat, o_mate, mask, occ_rims, occ_wide, virt_t,
    acc_own, acc_mate, acc_near, acc_third, abroad, sum_a, sum_b,
    in_sem, arg_sem, occ_ss, occ_rs, near_ss, near_rs, mate_ss, mate_rs, far_ss, far_rs, nsib_ss, nsib_rs, fsib_ss, fsib_rs,
    t_ss, t_rs, a_ss, a_rs, b_ss, b_rs,
):
    l, a = lax.axis_index("ao"), lax.axis_index("aux")
    zl, c = lax.div(a, 2), lax.rem(a, 2)
    zh = lax.rem(l, 2)
    flip = (1 - zl) * 2 + c
    twin = zl * 2 + 1 - c
    up, down = lax.rem(l + 1, n_ao), lax.rem(l + n_ao - 1, n_ao)
    mate = (l, flip)
    cross = (l + 1 - 2 * zh, flip)
    sib = (l, twin)
    onward = (lax.rem(l + n_ao + 2 - 4 * zh, n_ao), a)
    backward = (lax.rem(l + n_ao - 2 + 4 * zh, n_ao), a)
    n_b = 8
    n_a = n_ao // n_b
    ia, ib = lax.div(l, n_b), lax.rem(l, n_b)

    def peer_a(d):
        return lax.rem(ia + d, n_a) * n_b + ib

    def peer_b(d):
        return ia * n_b + lax.rem(ib + d, n_b)

    def copy(src, dst, ss, rs, to):
        return pltpu.make_async_remote_copy(
            src_ref=src, dst_ref=dst, send_sem=ss, recv_sem=rs, device_id=to, device_id_type=MESH
        )

    def load(g):
        return pltpu.make_async_copy(tensor_hbm.at[:, rows(g, GR), :], own_nat.at[:, rows(g, GR), :], in_sem.at[g])

    def send_near(g):
        return copy(own_row.at[rows(g, GR)], near.at[c, rows(g, GR)], near_ss.at[g], near_rs.at[g], cross)

    def send_mate(g):
        return copy(own_row.at[rows(g, GR)], mate_row.at[rows(g, GR)], mate_ss.at[g], mate_rs.at[g], mate)

    def send_far(g):
        return copy(near.at[c, rows(g, GR)], far.at[c, rows(g, GR)], far_ss.at[g], far_rs.at[g], onward)

    def near_sib(g, core):
        return copy(near.at[core, rows(g, GR)], near.at[core, rows(g, GR)], nsib_ss.at[g], nsib_rs.at[g], sib)

    def far_sib(g, core):
        return copy(far.at[core, rows(g, GR)], far.at[core, rows(g, GR)], fsib_ss.at[g], fsib_rs.at[g], sib)

    barrier = pltpu.get_barrier_semaphore()
    greeted = [mate, sib, (up, flip), (down, flip), onward, backward]
    greeted += [(peer_a(d), other) for d in range(1, n_a) for other in (a, twin, flip)]
    greeted += [(peer_b(d), a) for d in range(1, n_b)]
    for other in greeted:
        pl.semaphore_signal(barrier, inc=1, device_id=other, device_id_type=MESH)

    args = [
        pltpu.make_async_copy(src, dst, arg_sem.at[i])
        for i, (src, dst) in enumerate([(pattern_hbm, pattern), (occ_hbm, occ), (virt_hbm, virt)])
    ]
    for arg in args:
        arg.start()

    @pl.loop(0, NG)
    def _(g):
        load(g).start()

    args[0].wait()
    for p in range(PA):
        for o in range(3):
            kept = pattern[o, p].astype(F32)
            mask[p, :, o * AB : (o + 1) * AB] = jnp.full((GR, AB), kept, F32).astype(BF16)

    @pl.loop(0, NG)
    def _(g):
        load(g).wait()
        kept = own_nat[:, rows(g, GR), :] * mask[...]
        own_nat[:, rows(g, GR), :] = kept
        own_row[rows(g, GR)] = jnp.swapaxes(kept, 0, 1)

    args[1].wait()
    pl.semaphore_wait(barrier, len(greeted))

    to_up = copy(occ, occ_rims.at[0], occ_ss.at[0], occ_rs.at[0], (up, flip))
    to_down = copy(occ, occ_rims.at[1], occ_ss.at[1], occ_rs.at[1], (down, flip))
    to_up.start()
    to_down.start()

    @pl.loop(0, NG)
    def _(g):
        send_near(g).start()
        send_mate(g).start()

    args[2].wait()
    for j in range(3):
        virt_t[j] = virt[:, j * AB : (j + 1) * AB].astype(F32).T.astype(BF16)
    occ_wide[...] = jnp.zeros_like(occ_wide)
    occ_wide[AB:, AB:] = occ[...]
    for acc in (acc_own, acc_mate, acc_near, acc_third):
        acc[...] = jnp.zeros_like(acc)
    to_up.wait_recv()
    to_down.wait_recv()
    occ_wide[:AB, :W] = occ_rims[0]

    def occ_product(x):
        first = jnp.dot(x[:, : 2 * AB], occ_wide[...], preferred_element_type=F32)
        second = jnp.dot(x[:, 2 * AB :], occ_rims[1], preferred_element_type=F32)
        return jnp.concatenate(
            [first[:, : 2 * AB], first[:, 2 * AB :] + second[:, : 2 * AB], second[:, 2 * AB :]], axis=1
        ).astype(BF16)

    def virt_product(block, j, p):
        part = jnp.dot(virt_t[j], block[:, j * AB : j * AB + W], preferred_element_type=F32)
        t_nat[j, p] = part.astype(BF16)

    def to_rows(nat, dst, g):
        dst[rows(g, GR)] = jnp.swapaxes(nat[:, rows(g, GR), :], 0, 1)

    def pass_on(g):
        send_near(g).wait_recv()
        send_far(g).start()
        near_sib(g, c).start()

    @pl.loop(0, PA // PS)
    def _(s):
        product = occ_product(own_nat[rows(s, PS)].reshape(PS * AB, W))
        for q in range(PS):
            for j in range(3):
                virt_product(product[q * AB : (q + 1) * AB], j, s * PS + q)

    pass_on(0)

    @pl.loop(0, NG)
    def _(g):
        for j in range(3):
            to_rows(t_nat.at[j], t_own.at[j], g)

    share = copy(t_own.at[1], t_sib, t_ss, t_rs, sib)
    share.start()
    inward, outward = 2 - 2 * zh, 2 * zh
    t_in, t_out = t_own.at[inward], t_own.at[outward]
    m_in, m_out = t_mate.at[inward], t_mate.at[outward]
    t_pair = [t_own.at[1], t_sib]
    near_both = [near.at[0], near.at[1]]
    far_both = [far.at[0], far.at[1]]

    def take_far(g):
        send_far(g).wait_recv()
        far_sib(g, c).start()

    def use_far(g):
        far_sib(g, 1 - c).wait_recv()
        acc_near[...] += gram(side([t_out], g), side(far_both, g))

    pass_on(1)
    share.wait_recv()

    @pl.loop(0, NG)
    def _(g):
        @pl.when((g >= 1) & (g + 1 < NG))
        def _():
            pass_on(g + 1)

        acc_own[...] += gram(side(t_pair, g), side([own_row], g))
        near_sib(g, 1 - c).wait_recv()
        acc_near[...] += gram(side([t_in], g), side(near_both, g))
        send_mate(g).wait_recv()
        acc_mate[...] += gram(side(t_pair, g), side([mate_row], g))
        product = occ_product(mate_row[rows(g, GR)].reshape(GR * PA, W))
        o_mate[:, rows(g, GR), :] = jnp.swapaxes(product.reshape(GR, PA, 5 * AB), 0, 1)

        @pl.when(g >= 1)
        def _():
            take_far(g - 1)

        @pl.when(g >= 2)
        def _():
            use_far(g - 2)

    @pl.loop(0, PA // PS)
    def _(s):
        for q in range(PS):
            block = o_mate[s * PS + q]
            for j in (0, 2):
                virt_product(block, j, s * PS + q)

    @pl.loop(0, NG)
    def _(g):
        for j in (0, 2):
            to_rows(t_nat.at[j], t_mate.at[j], g)

    take_far(NG - 1)
    use_far(NG - 2)

    @pl.loop(0, NG // 2)
    def _(g):
        acc_third[...] += gram(side([m_in], g, 2 * GR), side(near_both, g, 2 * GR))

    use_far(NG - 1)

    @pl.loop(0, NG // 2)
    def _(g):
        acc_third[...] += gram(side([m_out], g, 2 * GR), side(far_both, g, 2 * GR))

    def pick(first, x, y):
        return jnp.where(first, jnp.concatenate([x, y], axis=1), jnp.concatenate([y, x], axis=1))

    none = jnp.zeros((PA, PA), F32)
    none_pair = jnp.zeros((PA, 2 * PA), F32)
    own_same, own_other = pick(c == 0, acc_own[:PA], none), pick(c == 0, acc_mate[:PA], none) + acc_near[...]
    sib_same, sib_other = pick(c == 0, acc_own[PA:], none), pick(c == 0, acc_mate[PA:], none)
    sum_a[ia] = folded(pick(zl == 0, own_same, own_other))
    abroad[0] = folded(pick(zl == 0, sib_same, sib_other))
    abroad[1] = folded(pick(zl == 0, none_pair, acc_third[...]))

    for d in range(n_a):
        copy(abroad.at[0], sum_a.at[n_a + ia], a_ss, a_rs, (peer_a(d), twin)).start()
        copy(abroad.at[1], sum_a.at[2 * n_a + ia], a_ss, a_rs, (peer_a(d), flip)).start()
        if d > 0:
            copy(sum_a.at[ia], sum_a.at[ia], a_ss, a_rs, (peer_a(d), a)).start()
    some = pl.ds(0, 3 * n_a - 1)
    all_a = copy(sum_a.at[some], sum_a.at[some], a_ss, a_rs, mate)
    all_a.wait_recv()
    part = sum_a[0]
    for i in range(1, 3 * n_a):
        part = part + sum_a[i]
    sum_b[ib] = part
    for d in range(1, n_b):
        copy(sum_b.at[ib], sum_b.at[ib], b_ss, b_rs, (peer_b(d), a)).start()
    some = pl.ds(0, n_b - 1)
    all_b = copy(sum_b.at[some], sum_b.at[some], b_ss, b_rs, (peer_b(1), a))
    all_b.wait_recv()
    total = sum_b[0]
    for i in range(1, n_b):
        total = total + sum_b[i]
    out[: PA // 2] = total[:, : 4 * PA]
    out[PA // 2 :] = total[:, 4 * PA :]

    to_up.wait_send()
    to_down.wait_send()
    share.wait_send()
    all_a.wait_send()
    all_b.wait_send()

    @pl.loop(0, NG)
    def _(g):
        send_near(g).wait_send()
        send_mate(g).wait_send()
        send_far(g).wait_send()
        near_sib(g, c).wait_send()
        far_sib(g, c).wait_send()


def solution(mesh):
    n_ao = mesh.shape["ao"]
    dma = pltpu.SemaphoreType.DMA
    row = (AB, PA, W)
    nat = (PA, AB, W)

    def on_device(tensor, pattern, occ, virt):
        buffers = [
            nat, row, row, (2, *row), (2, *row), row, (3, *row), (3, *row), (3, *nat), (PA, AB, 5 * AB),
            (PA, GR, W), (2, AB, W), (2 * AB, 4 * AB), (3, AB, AB),
        ]
        sums = [
            (2 * PA, PA), (2 * PA, PA), (PA, 2 * PA), (PA, 2 * PA), (2, 8, 128), (3 * n_ao // 8, 8, 128), (8, 8, 128),
        ]
        semaphores = [(NG,), (3,), (2,), (2,)] + [(NG,)] * 10 + [()] * 6
        return pl.pallas_call(
            functools.partial(kernel, n_ao),
            out_shape=jax.ShapeDtypeStruct((PA, 4 * PA), F32),
            in_specs=[pl.BlockSpec(memory_space=pltpu.HBM)] * 4,
            out_specs=pl.BlockSpec(memory_space=pltpu.VMEM),
            scratch_shapes=[
                pltpu.SMEM((3, PA), jnp.int32),
                pltpu.VMEM((AB, W), BF16),
                pltpu.VMEM((AB, W), BF16),
                *[pltpu.VMEM(shape, BF16) for shape in buffers],
                *[pltpu.VMEM(shape, F32) for shape in sums],
                *[dma(shape) for shape in semaphores],
            ],
            compiler_params=pltpu.CompilerParams(
                collective_id=0, has_side_effects=True, vmem_limit_bytes=60 << 20
            ),
        )(tensor, pattern.T, occ, virt)

    return jax.shard_map(
        on_device,
        mesh=mesh,
        in_specs=(P("aux", "ao", None), P("aux", "ao"), P("ao", None), P("ao", None)),
        out_specs=P("aux", None),
        check_vma=False,
    )
```

time: 77.6 us -> 70.4 us (0.907)
  Pallas kernels: 72.8 us -> 68.9 us
  local copies, waits for them, and re-layouts: 4.55 us -> 1.3 us
    pallas_call x1, Pallas kernels: 72.8 us -> 68.9 us  [on_device(): pl.pallas_call(functools.partial(kernel, n_ao), out_shape=jax.ShapeDtypeS...]
    unnamed x8 -> x1, local copies, waits for them, and re-layouts: 4.55 us -> 1.3 us
where the time goes in v2:
time: 70.4 us; the launch traced here: 70.2 us
  Pallas kernels  68.9 us (98%)
  local copies, waits for them, and re-layouts  1.3 us (2%)
    pallas_call x1, Pallas kernels, on_device(): pl.pallas_call(functools.partial(kernel, n_ao), out_shape=jax.ShapeDtypeS...  68.9 us

profile of v2, /device:TPU:0, one launch (start us, length us, event | category | flops | bytes accessed | tf_op | source)
XLA Modules:
  0.0 70.2 jit_solution(2030471122634936887)
XLA Ops:
  0.0 68.9 %shard_map.46 = f32[16,64]{1,0:T(8,128)} custom-call(bf16[16,128,384]{2,1,0:T(8,128)(2,1)} %tensor_hbm.1, s32[3,16]{1,0:T(4,128)} %bitcast.1, bf16[128,384]{1,0:T(8,128)(2,1)} %occ_hbm.1, bf16[128,384]{1,0:T(8,128)(2,1)} %virt_hbm.1), custom_call_target="tpu_custom_call" | custom-call | tf_op jit(solution)/shard_map/pallas_call | solution.py:311
  68.9 1.3 %copy.6 = f32[16,64]{1,0:T(8,128)} copy(f32[16,64]{1,0:T(8,128)} %shard_map.46) | data formatting | bytes 8192

commit v3 on v2

v3 whole, which is shorter than its diff:
```python
import functools

import jax
import jax.numpy as jnp
from jax import lax
from jax.experimental import pallas as pl
from jax.experimental.pallas import tpu as pltpu
from jax.sharding import PartitionSpec as P

MESH = pl.DeviceIdType.MESH
AB = 128
PA = 16
W = 3 * AB
NG = 8
GR = AB // NG
NC = 16
CR = AB // NC
LAST = 4
LR = CR // LAST
PS = 4
F32 = jnp.float32
BF16 = jnp.bfloat16


def rows(g, size):
    return pl.ds(pl.multiple_of(g * size, size), size)


def side(refs, g, count=GR):
    return jnp.concatenate(
        [jnp.concatenate([ref[g * count + u] for ref in refs], axis=0) for u in range(count)], axis=1
    )


def gram(left, right):
    return lax.dot_general(left, right, (((1,), (1,)), ((), ())), preferred_element_type=F32)


def folded(x):
    return jnp.concatenate([x[:8], x[8:]], axis=1)


def kernel(
    n_ao,
    tensor_hbm, pattern_hbm, occ_hbm, virt_hbm, out,
    pattern, occ, virt,
    own_nat, own_row, mate_row, near, far, t_sib, t_own, t_mate, t_nat, o_mate, mask, occ_rims, occ_wide, virt_t,
    acc_own, acc_mate, acc_cross, abroad, from_sib, sum_a, sum_b,
    in_sem, arg_sem, occ_ss, occ_rs, near_ss, near_rs, mate_ss, mate_rs, far_ss, far_rs, nsib_ss, nsib_rs, fsib_ss, fsib_rs,
    t_ss, t_rs, s_ss, s_rs, a_ss, a_rs, b_ss, b_rs,
):
    l, a = lax.axis_index("ao"), lax.axis_index("aux")
    zl, c = lax.div(a, 2), lax.rem(a, 2)
    zh = lax.rem(l, 2)
    flip = (1 - zl) * 2 + c
    twin = zl * 2 + 1 - c
    up, down = lax.rem(l + 1, n_ao), lax.rem(l + n_ao - 1, n_ao)
    mate = (l, flip)
    cross = (l + 1 - 2 * zh, flip)
    sib = (l, twin)
    onward = (lax.rem(l + n_ao + 2 - 4 * zh, n_ao), a)
    backward = (lax.rem(l + n_ao - 2 + 4 * zh, n_ao), a)
    n_x, n_y = n_ao // 8, 4
    ix, iy = lax.div(l, 8), lax.rem(lax.div(l, 2), 4)

    def peer(dx, dy):
        return (lax.rem(ix + dx, n_x) * n_y + lax.rem(iy + dy, n_y)) * 2 + zh

    def hops(d):
        return sum(min(step, n - step) for step, n in zip(d, (n_x, n_y)))

    far_first = sorted(((dx, dy) for dx in range(n_x) for dy in range(n_y) if dx + dy), key=hops, reverse=True)

    def copy(src, dst, ss, rs, to):
        return pltpu.make_async_remote_copy(
            src_ref=src, dst_ref=dst, send_sem=ss, recv_sem=rs, device_id=to, device_id_type=MESH
        )

    def load(g):
        return pltpu.make_async_copy(tensor_hbm.at[:, rows(g, GR), :], own_nat.at[:, rows(g, GR), :], in_sem.at[g])

    def piece(k):
        return rows(k, CR) if not isinstance(k, int) or k < NC - 1 else pl.ds((NC - 1) * CR + (k - NC + 1) * LR, LR)

    def send_near(k):
        return copy(own_row.at[piece(k)], near.at[c, piece(k)], near_ss.at[k], near_rs.at[k], cross)

    def send_mate(g):
        return copy(own_row.at[rows(g, GR)], mate_row.at[rows(g, GR)], mate_ss.at[g], mate_rs.at[g], mate)

    def send_far(k):
        return copy(near.at[c, piece(k)], far.at[c, piece(k)], far_ss.at[k], far_rs.at[k], onward)

    def near_sib(k, core):
        return copy(near.at[core, piece(k)], near.at[core, piece(k)], nsib_ss.at[k], nsib_rs.at[k], sib)

    def far_sib(k, core):
        return copy(far.at[core, piece(k)], far.at[core, piece(k)], fsib_ss.at[k], fsib_rs.at[k], sib)

    def rim(to):
        return copy(occ, occ_rims.at[c], occ_ss.at[0], occ_rs.at[0], to)

    def rim_sib(core):
        return copy(occ_rims.at[core], occ_rims.at[core], occ_ss.at[1], occ_rs.at[1], sib)

    barrier = pltpu.get_barrier_semaphore()
    greeted = [mate, sib, (up, flip), (down, flip), onward, backward]
    greeted += [(l + 1 - 2 * zh, a)] + [(peer(dx, dy), a) for dx, dy in far_first]
    for other in greeted:
        pl.semaphore_signal(barrier, inc=1, device_id=other, device_id_type=MESH)

    args = [
        pltpu.make_async_copy(src, dst, arg_sem.at[i])
        for i, (src, dst) in enumerate([(pattern_hbm, pattern), (occ_hbm, occ), (virt_hbm, virt)])
    ]
    for arg in args:
        arg.start()

    @pl.loop(0, NG)
    def _(g):
        load(g).start()

    args[0].wait()
    for p in range(PA):
        for o in range(3):
            kept = pattern[o, p].astype(F32)
            mask[p, :, o * AB : (o + 1) * AB] = jnp.full((GR, AB), kept, F32).astype(BF16)

    @pl.loop(0, NG)
    def _(g):
        load(g).wait()
        kept = own_nat[:, rows(g, GR), :] * mask[...]
        own_nat[:, rows(g, GR), :] = kept
        own_row[rows(g, GR)] = jnp.swapaxes(kept, 0, 1)

    args[1].wait()
    pl.semaphore_wait(barrier, len(greeted))

    rim_to = (lax.rem(l + n_ao + 1 - 2 * c, n_ao), flip)
    rim(rim_to).start()

    @pl.loop(0, NG - 1)
    def _(g):
        send_near(2 * g).start()
        send_near(2 * g + 1).start()
        send_mate(g).start()

    for k in range(NC - 2, NC - 1 + LAST):
        send_near(k).start()
    send_mate(NG - 1).start()

    args[2].wait()
    for j in range(3):
        virt_t[j] = virt[:, j * AB : (j + 1) * AB].astype(F32).T.astype(BF16)
    occ_wide[...] = jnp.zeros_like(occ_wide)
    occ_wide[AB:, AB:] = occ[...]
    for acc in (acc_own, acc_mate, acc_cross):
        acc[...] = jnp.zeros_like(acc)

    def occ_product(x):
        first = jnp.dot(x[:, : 2 * AB], occ_wide[...], preferred_element_type=F32)
        second = jnp.dot(x[:, 2 * AB :], occ_rims[1], preferred_element_type=F32)
        return jnp.concatenate(
            [first[:, : 2 * AB], first[:, 2 * AB :] + second[:, : 2 * AB], second[:, 2 * AB :]], axis=1
        ).astype(BF16)

    def virt_product(block, j, p):
        part = jnp.dot(virt_t[j], block[:, j * AB : j * AB + W], preferred_element_type=F32)
        t_nat[j, p] = part.astype(BF16)

    def to_rows(nat, dst, g):
        dst[rows(g, GR)] = jnp.swapaxes(nat[:, rows(g, GR), :], 0, 1)

    def pass_on(k):
        send_near(k).wait_recv()
        send_far(k).start()
        near_sib(k, c).start()

    def take_far(k):
        send_far(k).wait_recv()
        far_sib(k, c).start()

    inward, outward = 2 - 2 * zh, 2 * zh
    t_pair = [t_own.at[1], t_sib]
    near_both = [near.at[0], near.at[1]]
    far_both = [far.at[0], far.at[1]]
    share = copy(t_own.at[1], t_sib, t_ss, t_rs, sib)
    early = PA // PS

    def own_transform(s):
        product = occ_product(own_nat[rows(s, PS)].reshape(PS * AB, W))
        for q in range(PS):
            for j in range(3):
                virt_product(product[q * AB : (q + 1) * AB], j, s * PS + q)

    def mate_group(g):
        send_mate(g).wait_recv()
        product = occ_product(mate_row[rows(g, GR)].reshape(GR * PA, W))
        o_mate[:, rows(g, GR), :] = jnp.swapaxes(product.reshape(GR, PA, 5 * AB), 0, 1)
        acc_mate[...] += gram(side(t_pair, g), side([mate_row], g))

    @pl.loop(0, NC - 1)
    def _(k):
        pass_on(k)

        @pl.when(k >= 3)
        def _():
            take_far(k - 3)

        @pl.when(k == 0)
        def _():
            rim(rim_to).wait_recv()
            rim_sib(c).start()
            rim_sib(1 - c).wait_recv()
            occ_wide[:AB, :W] = occ_rims[0]

        @pl.when(k < early)
        def _():
            own_transform(k)

        @pl.when((k >= early) & (k < 2 * early))
        def _():
            for g in range(2):
                for j in range(3):
                    to_rows(t_nat.at[j], t_own.at[j], 2 * (k - early) + g)

        @pl.when(k == 2 * early - 1)
        def _():
            share.start()

        @pl.when(k == 2 * early)
        def _():
            share.wait_recv()

        @pl.when(k >= 2 * early)
        def _():
            mate_group(k - 2 * early)

        @pl.when((k >= 2 * early) & (k < 3 * early))
        def _():
            for g in range(2):
                at = 2 * (k - 2 * early) + g
                acc_own[...] += gram(side(t_pair, at), side([own_row], at))

    take_far(NC - 4)
    for k in range(NC - 1, NC - 1 + LAST):
        pass_on(k)
    mate_group(NG - 1)

    def pick(first, x, y):
        return jnp.where(first, jnp.concatenate([x, y], axis=1), jnp.concatenate([y, x], axis=1))

    none = jnp.zeros((PA, PA), F32)
    none_pair = jnp.zeros((PA, 2 * PA), F32)
    sib_same, sib_other = pick(c == 0, acc_own[PA:], none), pick(c == 0, acc_mate[PA:], none)
    abroad[0] = folded(pick(zl == 0, sib_same, sib_other))
    to_sib = copy(abroad.at[0], from_sib, s_ss, s_rs, sib)
    to_sib.start()

    for p in range(PA):
        block = o_mate[p]
        for j in (0, 2):
            virt_product(block, j, p)

    take_far(NC - 3)

    @pl.loop(0, NG)
    def _(g):
        for j in (0, 2):
            to_rows(t_nat.at[j], t_mate.at[j], g)

    def cross_gram(j, both, g, count):
        return gram(side([t_own.at[j], t_mate.at[j]], g, count), side(both, g, count))

    @pl.loop(0, NC - 1)
    def _(k):
        near_sib(k, 1 - c).wait_recv()

    for k in range(NC - 1, NC - 1 + LAST):
        near_sib(k, 1 - c).wait_recv()

    acc_cross[...] = cross_gram(inward, near_both, 0, AB // 2) + cross_gram(inward, near_both, 1, AB // 2)
    for k in range(NC - 2, NC - 1 + LAST):
        take_far(k)

    @pl.loop(0, NC - 4)
    def _(k):
        far_sib(k, 1 - c).wait_recv()

    acc_cross[...] += cross_gram(outward, far_both, 0, AB // 2) + cross_gram(outward, far_both, 2, AB // 4)
    for k in range(NC - 4, NC - 1 + LAST):
        far_sib(k, 1 - c).wait_recv()
    acc_cross[...] += cross_gram(outward, far_both, 3, AB // 4)

    own_same = pick(c == 0, acc_own[:PA], none)
    own_other = pick(c == 0, acc_mate[:PA], none) + acc_cross[:PA]
    abroad[1] = folded(pick(zl == 0, none_pair, acc_cross[PA:]))
    to_sib.wait_recv()
    sum_a[0] = folded(pick(zl == 0, own_same, own_other)) + from_sib[...]

    other_hi = l + 1 - 2 * zh
    copy(sum_a.at[0], sum_a.at[1], a_ss, a_rs, (other_hi, a)).start()
    copy(abroad.at[1], sum_a.at[2], a_ss, a_rs, cross).start()
    copy(abroad.at[1], sum_a.at[3], a_ss, a_rs, mate).start()
    some = pl.ds(0, 3)
    all_a = copy(sum_a.at[some], sum_a.at[some], a_ss, a_rs, mate)
    all_a.wait_recv()
    low, high = jnp.where(zh == 0, sum_a[0], sum_a[1]), jnp.where(zh == 0, sum_a[1], sum_a[0])
    low_third, high_third = jnp.where(zh == 0, sum_a[3], sum_a[2]), jnp.where(zh == 0, sum_a[2], sum_a[3])
    column = lax.div(l, 2)
    sum_b[column] = (low + low_third) + (high + high_third)
    for dx, dy in far_first:
        copy(sum_b.at[column], sum_b.at[column], b_ss, b_rs, (peer(dx, dy), a)).start()
    some = pl.ds(0, n_x * n_y - 1)
    all_b = copy(sum_b.at[some], sum_b.at[some], b_ss, b_rs, (peer(1, 0), a))
    all_b.wait_recv()
    total = sum_b[0]
    for i in range(1, n_x * n_y):
        total = total + sum_b[i]
    out[: PA // 2] = total[:, : 4 * PA]
    out[PA // 2 :] = total[:, 4 * PA :]

    rim(rim_to).wait_send()
    rim_sib(c).wait_send()
    share.wait_send()
    to_sib.wait_send()
    all_a.wait_send()
    all_b.wait_send()

    @pl.loop(0, NG)
    def _(g):
        send_mate(g).wait_send()

    def sent(k):
        send_near(k).wait_send()
        send_far(k).wait_send()
        near_sib(k, c).wait_send()
        far_sib(k, c).wait_send()

    pl.loop(0, NC - 1)(sent)
    for k in range(NC - 1, NC - 1 + LAST):
        sent(k)


def solution(mesh):
    n_ao = mesh.shape["ao"]
    dma = pltpu.SemaphoreType.DMA
    row = (AB, PA, W)
    nat = (PA, AB, W)

    def on_device(tensor, pattern, occ, virt):
        buffers = [
            nat, row, row, (2, *row), (2, *row), row, (3, *row), (3, *row), (3, *nat), (PA, AB, 5 * AB),
            (PA, GR, W), (2, AB, W), (2 * AB, 4 * AB), (3, AB, AB),
        ]
        sums = [
            (2 * PA, PA), (2 * PA, PA), (2 * PA, 2 * PA), (2, 8, 128), (8, 128), (4, 8, 128), (n_ao // 2, 8, 128),
        ]
        n_p = NC - 1 + LAST
        semaphores = [(NG,), (3,), (2,), (2,), (n_p,), (n_p,), (NG,), (NG,)] + [(n_p,)] * 6 + [()] * 8
        return pl.pallas_call(
            functools.partial(kernel, n_ao),
            out_shape=jax.ShapeDtypeStruct((PA, 4 * PA), F32),
            in_specs=[pl.BlockSpec(memory_space=pltpu.HBM)] * 4,
            out_specs=pl.BlockSpec(memory_space=pltpu.VMEM),
            scratch_shapes=[
                pltpu.SMEM((3, PA), jnp.int32),
                pltpu.VMEM((AB, W), BF16),
                pltpu.VMEM((AB, W), BF16),
                *[pltpu.VMEM(shape, BF16) for shape in buffers],
                *[pltpu.VMEM(shape, F32) for shape in sums],
                *[dma(shape) for shape in semaphores],
            ],
            compiler_params=pltpu.CompilerParams(
                collective_id=0, has_side_effects=True, vmem_limit_bytes=60 << 20
            ),
        )(tensor, pattern.T, occ, virt)

    return jax.shard_map(
        on_device,
        mesh=mesh,
        in_specs=(P("aux", "ao", None), P("aux", "ao"), P("ao", None), P("ao", None)),
        out_specs=P("aux", None),
        check_vma=False,
    )
```

time: 70.4 us -> 67.4 us (0.957)
  Pallas kernels: 68.9 us -> 65.9 us
    pallas_call x1, Pallas kernels: 68.9 us -> 65.9 us  [on_device(): pl.pallas_call(functools.partial(kernel, n_ao), out_shape=jax.ShapeDtypeS...]
where the time goes in v3:
time: 67.4 us; the launch traced here: 67.2 us
  Pallas kernels  65.9 us (98%)
  local copies, waits for them, and re-layouts  1.3 us (2%)
    pallas_call x1, Pallas kernels, on_device(): pl.pallas_call(functools.partial(kernel, n_ao), out_shape=jax.ShapeDtypeS...  65.9 us

profile of v3, /device:TPU:0, one launch (start us, length us, event | category | flops | bytes accessed | tf_op | source)
XLA Modules:
  0.0 67.2 jit_solution(10311387666024722300)
XLA Ops:
  0.0 65.9 %shard_map.46 = f32[16,64]{1,0:T(8,128)} custom-call(bf16[16,128,384]{2,1,0:T(8,128)(2,1)} %tensor_hbm.1, s32[3,16]{1,0:T(4,128)} %bitcast.1, bf16[128,384]{1,0:T(8,128)(2,1)} %occ_hbm.1, bf16[128,384]{1,0:T(8,128)(2,1)} %virt_hbm.1), custom_call_target="tpu_custom_call" | custom-call | tf_op jit(solution)/shard_map/pallas_call | solution.py:361
  65.9 1.3 %copy.6 = f32[16,64]{1,0:T(8,128)} copy(f32[16,64]{1,0:T(8,128)} %shard_map.46) | data formatting | bytes 8192

commit v4 on v3

--- a/solution.py
+++ b/solution.py
@@ -45,16 +45,15 @@
     tensor_hbm, pattern_hbm, occ_hbm, virt_hbm, out,
     pattern, occ, virt,
     own_nat, own_row, mate_row, near, far, t_sib, t_own, t_mate, t_nat, o_mate, mask, occ_rims, occ_wide, virt_t,
-    acc_own, acc_mate, acc_cross, abroad, from_sib, sum_a, sum_b,
-    in_sem, arg_sem, occ_ss, occ_rs, near_ss, near_rs, mate_ss, mate_rs, far_ss, far_rs, nsib_ss, nsib_rs, fsib_ss, fsib_rs,
-    t_ss, t_rs, s_ss, s_rs, a_ss, a_rs, b_ss, b_rs,
+    acc_own, acc_mate, acc_cross, for_sib, from_sib, third, sums,
+    in_sem, arg_sem, rim_ss, rim_rs, near_ss, near_rs, mate_ss, mate_rs, far_ss, far_rs, nsib_ss, nsib_rs, fsib_ss, fsib_rs,
+    t_ss, t_rs, s_ss, s_rs, sum_ss, sum_rs, entered,
 ):
     l, a = lax.axis_index("ao"), lax.axis_index("aux")
     zl, c = lax.div(a, 2), lax.rem(a, 2)
     zh = lax.rem(l, 2)
     flip = (1 - zl) * 2 + c
     twin = zl * 2 + 1 - c
-    up, down = lax.rem(l + 1, n_ao), lax.rem(l + n_ao - 1, n_ao)
     mate = (l, flip)
     cross = (l + 1 - 2 * zh, flip)
     sib = (l, twin)
@@ -63,13 +62,16 @@
     n_x, n_y = n_ao // 8, 4
     ix, iy = lax.div(l, 8), lax.rem(lax.div(l, 2), 4)
 
-    def peer(dx, dy):
-        return (lax.rem(ix + dx, n_x) * n_y + lax.rem(iy + dy, n_y)) * 2 + zh
-
-    def hops(d):
-        return sum(min(step, n - step) for step, n in zip(d, (n_x, n_y)))
-
-    far_first = sorted(((dx, dy) for dx in range(n_x) for dy in range(n_y) if dx + dy), key=hops, reverse=True)
+    def peer(step):
+        dx, dy, dz = step[:3]
+        return (lax.rem(ix + dx, n_x) * n_y + lax.rem(iy + dy, n_y)) * 2 + lax.rem(zh + dz, 2)
+
+    def hops(step):
+        dx, dy, dz, other = step
+        return min(dx, n_x - dx) + min(dy, n_y - dy) + (1 if other else 2 * dz)
+
+    steps = [(dx, dy, dz, other) for dx in range(n_x) for dy in range(n_y) for dz in range(2) for other in range(2)]
+    far_first = sorted((step for step in steps if sum(step)), key=hops, reverse=True)
 
     def copy(src, dst, ss, rs, to):
         return pltpu.make_async_remote_copy(
@@ -97,15 +99,24 @@
     def far_sib(k, core):
         return copy(far.at[core, piece(k)], far.at[core, piece(k)], fsib_ss.at[k], fsib_rs.at[k], sib)
 
-    def rim(to):
-        return copy(occ, occ_rims.at[c], occ_ss.at[0], occ_rs.at[0], to)
-
-    def rim_sib(core):
-        return copy(occ_rims.at[core], occ_rims.at[core], occ_ss.at[1], occ_rs.at[1], sib)
+    half = rows(c, AB // 2)
+
+    def rim_in():
+        return copy(occ.at[half], occ_rims.at[zh, half], rim_ss.at[0], rim_rs.at[0], cross)
+
+    def rim_out():
+        return copy(occ_rims.at[1 - zh, half], occ_rims.at[zh, half], rim_ss.at[1], rim_rs.at[1], onward)
+
+    def rim_sib(outer, core):
+        at = (zh if outer else 1 - zh), rows(core, AB // 2)
+        return copy(occ_rims.at[at], occ_rims.at[at], rim_ss.at[2 + outer], rim_rs.at[2 + outer], sib)
 
     barrier = pltpu.get_barrier_semaphore()
-    greeted = [mate, sib, (up, flip), (down, flip), onward, backward]
-    greeted += [(l + 1 - 2 * zh, a)] + [(peer(dx, dy), a) for dx, dy in far_first]
+    def across(bit):
+        return l + bit * (1 - 2 * lax.rem(lax.div(l, bit), 2)), a
+
+    halves = [mate] + [across(bit) for bit in (1, 2, 4, 8, 16)]
+    greeted = [sib, cross, onward, backward, *halves]
     for other in greeted:
         pl.semaphore_signal(barrier, inc=1, device_id=other, device_id_type=MESH)
 
@@ -136,8 +147,7 @@
     args[1].wait()
     pl.semaphore_wait(barrier, len(greeted))
 
-    rim_to = (lax.rem(l + n_ao + 1 - 2 * c, n_ao), flip)
-    rim(rim_to).start()
+    rim_in().start()
 
     @pl.loop(0, NG - 1)
     def _(g):
@@ -193,12 +203,22 @@
             for j in range(3):
                 virt_product(product[q * AB : (q + 1) * AB], j, s * PS + q)
 
+    def own_rows(g):
+        for j in range(3):
+            to_rows(t_nat.at[j], t_own.at[j], g)
+
     def mate_group(g):
         send_mate(g).wait_recv()
         product = occ_product(mate_row[rows(g, GR)].reshape(GR * PA, W))
         o_mate[:, rows(g, GR), :] = jnp.swapaxes(product.reshape(GR, PA, 5 * AB), 0, 1)
         acc_mate[...] += gram(side(t_pair, g), side([mate_row], g))
 
+    def own_group(g):
+        acc_own[...] += gram(side(t_pair, g), side([own_row], g))
+
+    def at(k, first, last=None):
+        return pl.when(k == first if last is None else (k >= first) & (k <= last))
+
     @pl.loop(0, NC - 1)
     def _(k):
         pass_on(k)
@@ -206,41 +226,66 @@
         @pl.when(k >= 3)
         def _():
             take_far(k - 3)
-
-        @pl.when(k == 0)
-        def _():
-            rim(rim_to).wait_recv()
-            rim_sib(c).start()
-            rim_sib(1 - c).wait_recv()
+            near_sib(k - 3, 1 - c).wait_recv()
+
+        @pl.when(k >= 6)
+        def _():
+            far_sib(k - 6, 1 - c).wait_recv()
+
+        for i, other in enumerate(halves):
+
+            @at(k, 2 * i + 1)
+            def _(i=i, other=other):
+                pl.semaphore_signal(entered.at[i], inc=1, device_id=other, device_id_type=MESH)
+
+            @at(k, 2 * i + 2)
+            def _(i=i):
+                pl.semaphore_wait(entered.at[i], 1)
+
+        @at(k, 0)
+        def _():
+            rim_in().wait_recv()
+            rim_out().start()
+            rim_sib(0, c).start()
+
+        @at(k, 1)
+        def _():
+            rim_out().wait_recv()
+            rim_sib(1, c).start()
+            rim_sib(0, 1 - c).wait_recv()
+            rim_sib(1, 1 - c).wait_recv()
             occ_wide[:AB, :W] = occ_rims[0]
 
-        @pl.when(k < early)
-        def _():
-            own_transform(k)
-
-        @pl.when((k >= early) & (k < 2 * early))
-        def _():
-            for g in range(2):
-                for j in range(3):
-                    to_rows(t_nat.at[j], t_own.at[j], 2 * (k - early) + g)
-
-        @pl.when(k == 2 * early - 1)
+        @at(k, 2, 5)
+        def _():
+            own_transform(k - 2)
+
+        @at(k, 6, 8)
+        def _():
+            own_rows(3 * (k - 6))
+            own_rows(3 * (k - 6) + 1)
+
+        @at(k, 6, 7)
+        def _():
+            own_rows(3 * (k - 6) + 2)
+
+        @at(k, 8)
         def _():
             share.start()
 
-        @pl.when(k == 2 * early)
+        @at(k, 9)
         def _():
             share.wait_recv()
-
-        @pl.when(k >= 2 * early)
-        def _():
-            mate_group(k - 2 * early)
-
-        @pl.when((k >= 2 * early) & (k < 3 * early))
-        def _():
-            for g in range(2):
-                at = 2 * (k - 2 * early) + g
-                acc_own[...] += gram(side(t_pair, at), side([own_row], at))
+            mate_group(0)
+
+        @at(k, 9, 14)
+        def _():
+            mate_group(k - 8)
+
+        @at(k, 10, 13)
+        def _():
+            own_group(2 * (k - 10))
+            own_group(2 * (k - 10) + 1)
 
     take_far(NC - 4)
     for k in range(NC - 1, NC - 1 + LAST):
@@ -253,8 +298,8 @@
     none = jnp.zeros((PA, PA), F32)
     none_pair = jnp.zeros((PA, 2 * PA), F32)
     sib_same, sib_other = pick(c == 0, acc_own[PA:], none), pick(c == 0, acc_mate[PA:], none)
-    abroad[0] = folded(pick(zl == 0, sib_same, sib_other))
-    to_sib = copy(abroad.at[0], from_sib, s_ss, s_rs, sib)
+    for_sib[...] = folded(pick(zl == 0, sib_same, sib_other))
+    to_sib = copy(for_sib, from_sib, s_ss, s_rs, sib)
     to_sib.start()
 
     for p in range(PA):
@@ -272,21 +317,14 @@
     def cross_gram(j, both, g, count):
         return gram(side([t_own.at[j], t_mate.at[j]], g, count), side(both, g, count))
 
-    @pl.loop(0, NC - 1)
-    def _(k):
-        near_sib(k, 1 - c).wait_recv()
-
-    for k in range(NC - 1, NC - 1 + LAST):
+    for k in range(NC - 4, NC - 1 + LAST):
         near_sib(k, 1 - c).wait_recv()
 
     acc_cross[...] = cross_gram(inward, near_both, 0, AB // 2) + cross_gram(inward, near_both, 1, AB // 2)
     for k in range(NC - 2, NC - 1 + LAST):
         take_far(k)
-
-    @pl.loop(0, NC - 4)
-    def _(k):
+    for k in range(NC - 7, NC - 4):
         far_sib(k, 1 - c).wait_recv()
-
     acc_cross[...] += cross_gram(outward, far_both, 0, AB // 2) + cross_gram(outward, far_both, 2, AB // 4)
     for k in range(NC - 4, NC - 1 + LAST):
         far_sib(k, 1 - c).wait_recv()
@@ -294,42 +332,16 @@
 
     own_same = pick(c == 0, acc_own[:PA], none)
     own_other = pick(c == 0, acc_mate[:PA], none) + acc_cross[:PA]
-    abroad[1] = folded(pick(zl == 0, none_pair, acc_cross[PA:]))
+    third[...] = folded(pick(zl == 0, none_pair, acc_cross[PA:]))
     to_sib.wait_recv()
-    sum_a[0] = folded(pick(zl == 0, own_same, own_other)) + from_sib[...]
-
-    other_hi = l + 1 - 2 * zh
-    copy(sum_a.at[0], sum_a.at[1], a_ss, a_rs, (other_hi, a)).start()
-    copy(abroad.at[1], sum_a.at[2], a_ss, a_rs, cross).start()
-    copy(abroad.at[1], sum_a.at[3], a_ss, a_rs, mate).start()
-    some = pl.ds(0, 3)
-    all_a = copy(sum_a.at[some], sum_a.at[some], a_ss, a_rs, mate)
-    all_a.wait_recv()
-    low, high = jnp.where(zh == 0, sum_a[0], sum_a[1]), jnp.where(zh == 0, sum_a[1], sum_a[0])
-    low_third, high_third = jnp.where(zh == 0, sum_a[3], sum_a[2]), jnp.where(zh == 0, sum_a[2], sum_a[3])
-    column = lax.div(l, 2)
-    sum_b[column] = (low + low_third) + (high + high_third)
-    for dx, dy in far_first:
-        copy(sum_b.at[column], sum_b.at[column], b_ss, b_rs, (peer(dx, dy), a)).start()
-    some = pl.ds(0, n_x * n_y - 1)
-    all_b = copy(sum_b.at[some], sum_b.at[some], b_ss, b_rs, (peer(1, 0), a))
-    all_b.wait_recv()
-    total = sum_b[0]
-    for i in range(1, n_x * n_y):
-        total = total + sum_b[i]
-    out[: PA // 2] = total[:, : 4 * PA]
-    out[PA // 2 :] = total[:, 4 * PA :]
-
-    rim(rim_to).wait_send()
-    rim_sib(c).wait_send()
-    share.wait_send()
-    to_sib.wait_send()
-    all_a.wait_send()
-    all_b.wait_send()
-
-    @pl.loop(0, NG)
-    def _(g):
-        send_mate(g).wait_send()
+    sums[l] = folded(pick(zl == 0, own_same, own_other)) + from_sib[...]
+
+    def piece_to(step):
+        src, slot, aux = (third, n_ao + l, flip) if step[3] else (sums.at[l], l, a)
+        return copy(src, sums.at[slot], sum_ss, sum_rs, (peer(step), aux))
+
+    for step in far_first:
+        piece_to(step).start()
 
     def sent(k):
         send_near(k).wait_send()
@@ -340,6 +352,23 @@
     pl.loop(0, NC - 1)(sent)
     for k in range(NC - 1, NC - 1 + LAST):
         sent(k)
+
+    @pl.loop(0, NG)
+    def _(g):
+        send_mate(g).wait_send()
+
+    for sent_rim in (rim_in(), rim_out(), rim_sib(0, c), rim_sib(1, c), share, to_sib):
+        sent_rim.wait_send()
+
+    most = pl.ds(0, 2 * n_ao - 1)
+    everything = copy(sums.at[most], sums.at[most], sum_ss, sum_rs, mate)
+    everything.wait_recv()
+    total = [sums[i] for i in range(2 * n_ao)]
+    while len(total) > 1:
+        total = [x + y for x, y in zip(total[::2], total[1::2])]
+    out[: PA // 2] = total[0][:, : 4 * PA]
+    out[PA // 2 :] = total[0][:, 4 * PA :]
+    everything.wait_send()
 
 
 def solution(mesh):
@@ -354,10 +383,10 @@
             (PA, GR, W), (2, AB, W), (2 * AB, 4 * AB), (3, AB, AB),
         ]
         sums = [
-            (2 * PA, PA), (2 * PA, PA), (2 * PA, 2 * PA), (2, 8, 128), (8, 128), (4, 8, 128), (n_ao // 2, 8, 128),
+            (2 * PA, PA), (2 * PA, PA), (2 * PA, 2 * PA), (8, 128), (8, 128), (8, 128), (2 * n_ao, 8, 128),
         ]
         n_p = NC - 1 + LAST
-        semaphores = [(NG,), (3,), (2,), (2,), (n_p,), (n_p,), (NG,), (NG,)] + [(n_p,)] * 6 + [()] * 8
+        semaphores = [(NG,), (3,), (4,), (4,), (n_p,), (n_p,), (NG,), (NG,)] + [(n_p,)] * 6 + [()] * 6
         return pl.pallas_call(
             functools.partial(kernel, n_ao),
             out_shape=jax.ShapeDtypeStruct((PA, 4 * PA), F32),
@@ -370,6 +399,7 @@
                 *[pltpu.VMEM(shape, BF16) for shape in buffers],
                 *[pltpu.VMEM(shape, F32) for shape in sums],
                 *[dma(shape) for shape in semaphores],
+                pltpu.SemaphoreType.REGULAR((6,)),
             ],
             compiler_params=pltpu.CompilerParams(
                 collective_id=0, has_side_effects=True, vmem_limit_bytes=60 << 20

time: 67.4 us -> 63.2 us (0.938)
  Pallas kernels: 65.9 us -> 61.1 us
    pallas_call x1, Pallas kernels: 65.9 us -> 61.1 us  [on_device(): pl.pallas_call(functools.partial(kernel, n_ao), out_shape=jax.ShapeDtypeS...]
where the time goes in v4:
time: 63.2 us; the launch traced here: 62.4 us
  Pallas kernels  61.1 us (97%)
  local copies, waits for them, and re-layouts  1.3 us (2%)
    pallas_call x1, Pallas kernels, on_device(): pl.pallas_call(functools.partial(kernel, n_ao), out_shape=jax.ShapeDtypeS...  61.1 us
    unnamed x1, local copies, waits for them, and re-layouts  1.3 us

profile of v4, /device:TPU:0, one launch (start us, length us, event | category | flops | bytes accessed | tf_op | source)
XLA Modules:
  0.0 62.4 jit_solution(15369925696157223780)
XLA Ops:
  0.0 61.1 %shard_map.46 = f32[16,64]{1,0:T(8,128)} custom-call(bf16[16,128,384]{2,1,0:T(8,128)(2,1)} %tensor_hbm.1, s32[3,16]{1,0:T(4,128)} %bitcast.1, bf16[128,384]{1,0:T(8,128)(2,1)} %occ_hbm.1, bf16[128,384]{1,0:T(8,128)(2,1)} %virt_hbm.1), custom_call_target="tpu_custom_call" | custom-call | tf_op jit(solution)/shard_map/pallas_call | solution.py:390
  61.1 1.3 %copy.6 = f32[16,64]{1,0:T(8,128)} copy(f32[16,64]{1,0:T(8,128)} %shard_map.46) | data formatting | bytes 8192

commit v5 on v4

--- a/solution.py
+++ b/solution.py
@@ -137,25 +137,38 @@
             kept = pattern[o, p].astype(F32)
             mask[p, :, o * AB : (o + 1) * AB] = jnp.full((GR, AB), kept, F32).astype(BF16)
 
-    @pl.loop(0, NG)
-    def _(g):
+    def mask_group(g):
         load(g).wait()
         kept = own_nat[:, rows(g, GR), :] * mask[...]
         own_nat[:, rows(g, GR), :] = kept
         own_row[rows(g, GR)] = jnp.swapaxes(kept, 0, 1)
 
+    def send_group(g):
+        send_near(2 * g).start()
+
+        @pl.when(g < NG - 1)
+        def _():
+            send_near(2 * g + 1).start()
+
+        @pl.when(g < NG - 1)
+        def _():
+            send_mate(g).start()
+
+    ahead = 2
+    pl.loop(0, ahead)(mask_group)
     args[1].wait()
     pl.semaphore_wait(barrier, len(greeted))
-
     rim_in().start()
 
-    @pl.loop(0, NG - 1)
+    @pl.loop(0, NG)
     def _(g):
-        send_near(2 * g).start()
-        send_near(2 * g + 1).start()
-        send_mate(g).start()
-
-    for k in range(NC - 2, NC - 1 + LAST):
+        send_group(g)
+
+        @pl.when(g < NG - ahead)
+        def _():
+            mask_group(g + ahead)
+
+    for k in range(NC - 1, NC - 1 + LAST):
         send_near(k).start()
     send_mate(NG - 1).start()
 
@@ -219,18 +232,26 @@
     def at(k, first, last=None):
         return pl.when(k == first if last is None else (k >= first) & (k <= last))
 
-    @pl.loop(0, NC - 1)
+    @pl.loop(0, NC)
     def _(k):
-        pass_on(k)
-
-        @pl.when(k >= 3)
+        @pl.when(k < NC - 1)
+        def _():
+            pass_on(k)
+
+        @pl.when((k >= 3) & (k < NC - 1))
         def _():
             take_far(k - 3)
             near_sib(k - 3, 1 - c).wait_recv()
 
-        @pl.when(k >= 6)
+        @pl.when((k >= 6) & (k < NC - 1))
         def _():
             far_sib(k - 6, 1 - c).wait_recv()
+
+        @at(k, NC - 1)
+        def _():
+            take_far(NC - 4)
+            for last in range(NC - 1, NC - 1 + LAST):
+                pass_on(last)
 
         for i, other in enumerate(halves):
 
@@ -262,12 +283,7 @@
 
         @at(k, 6, 8)
         def _():
-            own_rows(3 * (k - 6))
-            own_rows(3 * (k - 6) + 1)
-
-        @at(k, 6, 7)
-        def _():
-            own_rows(3 * (k - 6) + 2)
+            pl.loop(3 * (k - 6), jnp.minimum(3 * (k - 6) + 3, NG))(own_rows)
 
         @at(k, 8)
         def _():
@@ -276,21 +292,14 @@
         @at(k, 9)
         def _():
             share.wait_recv()
-            mate_group(0)
-
-        @at(k, 9, 14)
-        def _():
-            mate_group(k - 8)
+
+        @at(k, 9, NC - 1)
+        def _():
+            pl.loop(jnp.where(k == 9, 0, k - 8), k - 7)(mate_group)
 
         @at(k, 10, 13)
         def _():
-            own_group(2 * (k - 10))
-            own_group(2 * (k - 10) + 1)
-
-    take_far(NC - 4)
-    for k in range(NC - 1, NC - 1 + LAST):
-        pass_on(k)
-    mate_group(NG - 1)
+            pl.loop(2 * (k - 10), 2 * (k - 10) + 2)(own_group)
 
     def pick(first, x, y):
         return jnp.where(first, jnp.concatenate([x, y], axis=1), jnp.concatenate([y, x], axis=1))
@@ -302,10 +311,12 @@
     to_sib = copy(for_sib, from_sib, s_ss, s_rs, sib)
     to_sib.start()
 
-    for p in range(PA):
-        block = o_mate[p]
-        for j in (0, 2):
-            virt_product(block, j, p)
+    @pl.loop(0, PA // 8)
+    def _(s):
+        for q in range(8):
+            block = o_mate[8 * s + q]
+            for j in (0, 2):
+                virt_product(block, j, 8 * s + q)
 
     take_far(NC - 3)
 
@@ -320,7 +331,10 @@
     for k in range(NC - 4, NC - 1 + LAST):
         near_sib(k, 1 - c).wait_recv()
 
-    acc_cross[...] = cross_gram(inward, near_both, 0, AB // 2) + cross_gram(inward, near_both, 1, AB // 2)
+    @pl.loop(0, 2)
+    def _(g):
+        acc_cross[...] += cross_gram(inward, near_both, g, AB // 2)
+
     for k in range(NC - 2, NC - 1 + LAST):
         take_far(k)
     for k in range(NC - 7, NC - 4):
@@ -402,7 +416,7 @@
                 pltpu.SemaphoreType.REGULAR((6,)),
             ],
             compiler_params=pltpu.CompilerParams(
-                collective_id=0, has_side_effects=True, vmem_limit_bytes=60 << 20
+                collective_id=0, has_side_effects=True, vmem_limit_bytes=55200 << 10
             ),
         )(tensor, pattern.T, occ, virt)
 

time: 63.2 us -> 61.7 us (0.976)
  Pallas kernels: 61.1 us -> 59.9 us
    pallas_call x1, Pallas kernels: 61.1 us -> 59.9 us  [on_device(): pl.pallas_call(functools.partial(kernel, n_ao), out_shape=jax.ShapeDtypeS...]
    unnamed x1 -> x3, local copies, waits for them, and re-layouts: 1.3 us -> 1.28 us
where the time goes in v5:
time: 61.7 us; the launch traced here: 61.1 us
  Pallas kernels  59.9 us (97%)
  local copies, waits for them, and re-layouts  1.28 us (2%)
    pallas_call x1, Pallas kernels, on_device(): pl.pallas_call(functools.partial(kernel, n_ao), out_shape=jax.ShapeDtypeS...  59.9 us
    unnamed x3, local copies, waits for them, and re-layouts  1.28 us

profile of v5, /device:TPU:0, one launch (start us, length us, event | category | flops | bytes accessed | tf_op | source)
XLA Modules:
  0.0 61.1 jit_solution(5382713431706078922)
XLA Ops:
  0.0 0.0 copy-start
  0.0 0.7 %copy-done = s32[16,3]{0,1:T(4,128)S(1)} copy-done((s32[16,3]{0,1:T(4,128)S(1)}, s32[16,3]{0,1:T(4,128)}, u32[]{:S(2)}) %copy-start) | copy-done | bytes 216
  0.7 59.9 %shard_map.46 = f32[16,64]{1,0:T(8,128)S(1)} custom-call(bf16[16,128,384]{2,1,0:T(8,128)(2,1)} %tensor_hbm.1, s32[3,16]{1,0:T(4,128)S(1)} %bitcast.1, bf16[128,384]{1,0:T(8,128)(2,1)} %occ_hbm.1, bf16[128,384]{1,0:T(8,128)(2,1)} %virt_hbm.1), custom_call_target="tpu_custom_call" | custom-call | tf_op jit(solution)/shard_map/pallas_call | solution.py:404
  60.5 0.6 copy.6
Async XLA Ops:
  0.0 0.7 %copy-start = (s32[16,3]{0,1:T(4,128)S(1)}, s32[16,3]{0,1:T(4,128)}, u32[]{:S(2)}) copy-start(s32[16,3]{0,1:T(4,128)} %param.5) | copy-start | bytes 580

commit v6 on v5

--- a/solution.py
+++ b/solution.py
@@ -150,9 +150,9 @@
         def _():
             send_near(2 * g + 1).start()
 
-        @pl.when(g < NG - 1)
-        def _():
-            send_mate(g).start()
+        @pl.when(g > 0)
+        def _():
+            send_mate(g - 1).start()
 
     ahead = 2
     pl.loop(0, ahead)(mask_group)
@@ -335,7 +335,11 @@
     def _(g):
         acc_cross[...] += cross_gram(inward, near_both, g, AB // 2)
 
-    for k in range(NC - 2, NC - 1 + LAST):
+        @pl.when(g == 0)
+        def _():
+            take_far(NC - 2)
+
+    for k in range(NC - 1, NC - 1 + LAST):
         take_far(k)
     for k in range(NC - 7, NC - 4):
         far_sib(k, 1 - c).wait_recv()

time: 61.7 us -> 61.7 us (level)
  no operation moved by 1% of the time
where the time goes in v6:
time: 61.7 us; the launch traced here: 61.1 us
  Pallas kernels  59.9 us (97%)
  local copies, waits for them, and re-layouts  1.28 us (2%)
    pallas_call x1, Pallas kernels, on_device(): pl.pallas_call(functools.partial(kernel, n_ao), out_shape=jax.ShapeDtypeS...  59.9 us
    unnamed x3, local copies, waits for them, and re-layouts  1.28 us

profile of v6, /device:TPU:0, one launch (start us, length us, event | category | flops | bytes accessed | tf_op | source)
XLA Modules:
  0.0 61.1 jit_solution(14401798232235639971)
XLA Ops:
  0.0 0.0 copy-start
  0.0 0.7 %copy-done = s32[16,3]{0,1:T(4,128)S(1)} copy-done((s32[16,3]{0,1:T(4,128)S(1)}, s32[16,3]{0,1:T(4,128)}, u32[]{:S(2)}) %copy-start) | copy-done | bytes 216
  0.7 59.9 %shard_map.46 = f32[16,64]{1,0:T(8,128)S(1)} custom-call(bf16[16,128,384]{2,1,0:T(8,128)(2,1)} %tensor_hbm.1, s32[3,16]{1,0:T(4,128)S(1)} %bitcast.1, bf16[128,384]{1,0:T(8,128)(2,1)} %occ_hbm.1, bf16[128,384]{1,0:T(8,128)(2,1)} %virt_hbm.1), custom_call_target="tpu_custom_call" | custom-call | tf_op jit(solution)/shard_map/pallas_call | solution.py:408
  60.5 0.6 copy.6
Async XLA Ops:
  0.0 0.7 %copy-start = (s32[16,3]{0,1:T(4,128)S(1)}, s32[16,3]{0,1:T(4,128)}, u32[]{:S(2)}) copy-start(s32[16,3]{0,1:T(4,128)} %param.5) | copy-start | bytes 580

commit v7 on v5

--- a/solution.py
+++ b/solution.py
@@ -71,7 +71,7 @@
         return min(dx, n_x - dx) + min(dy, n_y - dy) + (1 if other else 2 * dz)
 
     steps = [(dx, dy, dz, other) for dx in range(n_x) for dy in range(n_y) for dz in range(2) for other in range(2)]
-    far_first = sorted((step for step in steps if sum(step)), key=hops, reverse=True)
+    far_first = sorted((step for step in steps if sum(step)), key=lambda step: (hops(step), step[3]), reverse=True)
 
     def copy(src, dst, ss, rs, to):
         return pltpu.make_async_remote_copy(

time: 61.7 us -> 61.9 us (level)
  no operation moved by 1% of the time
where the time goes in v7:
time: 61.9 us; the launch traced here: 61 us
  Pallas kernels  59.7 us (96%)
  local copies, waits for them, and re-layouts  1.28 us (2%)
    pallas_call x1, Pallas kernels, on_device(): pl.pallas_call(functools.partial(kernel, n_ao), out_shape=jax.ShapeDtypeS...  59.7 us
    unnamed x3, local copies, waits for them, and re-layouts  1.28 us

profile of v7, /device:TPU:0, one launch (start us, length us, event | category | flops | bytes accessed | tf_op | source)
XLA Modules:
  0.0 61.0 jit_solution(1148436497825070460)
XLA Ops:
  0.0 0.0 copy-start
  0.0 0.7 %copy-done = s32[16,3]{0,1:T(4,128)S(1)} copy-done((s32[16,3]{0,1:T(4,128)S(1)}, s32[16,3]{0,1:T(4,128)}, u32[]{:S(2)}) %copy-start) | copy-done | bytes 216
  0.7 59.7 %shard_map.46 = f32[16,64]{1,0:T(8,128)S(1)} custom-call(bf16[16,128,384]{2,1,0:T(8,128)(2,1)} %tensor_hbm.1, s32[3,16]{1,0:T(4,128)S(1)} %bitcast.1, bf16[128,384]{1,0:T(8,128)(2,1)} %occ_hbm.1, bf16[128,384]{1,0:T(8,128)(2,1)} %virt_hbm.1), custom_call_target="tpu_custom_call" | custom-call | tf_op jit(solution)/shard_map/pallas_call | solution.py:404
  60.4 0.6 copy.6
Async XLA Ops:
  0.0 0.7 %copy-start = (s32[16,3]{0,1:T(4,128)S(1)}, s32[16,3]{0,1:T(4,128)}, u32[]{:S(2)}) copy-start(s32[16,3]{0,1:T(4,128)} %param.5) | copy-start | bytes 580
